TPU v7x, 32 devices: a whole 2x2x4 slice. The times are simulated.
32 devices in a mesh: seq: 8 (over y, x, core), head: 4 (over z).
Axes of the slice: x: 2, y: 2, z: 4, core: 2. Of those that a mesh axis runs over, the one named last changes fastest.
Arguments:
- tokens: bfloat16 [2, 2, 4096, 1536], P(None, None, 'seq'), may hold values from -6 to 6
- norm_gain: float32 [1536], replicated, may hold values from 0.1 to 1.9
- w_z: bfloat16 [1536, 3072], P('seq', 'head'), may hold values from -0.15625 to 0.15625
- w_x: bfloat16 [1536, 3072], P('seq', 'head'), may hold values from -0.15625 to 0.15625
- w_bc: bfloat16 [1536, 256], P('seq'), may hold values from -0.15625 to 0.15625
- w_dt: bfloat16 [1536, 48], P('seq', 'head'), may hold values from -0.15625 to 0.15625
- conv_x: float32 [4, 3072], P(None, 'head'), may hold values from -3 to 3
- conv_x_bias: float32 [3072], P('head'), may hold values from -2 to 2
- conv_bc: float32 [4, 256], replicated, may hold values from -3 to 3
- conv_bc_bias: float32 [256], replicated, may hold values from -2 to 2
- dt_bias: float32 [48], P('head'), may hold values from -6 to -2
- a_log: float32 [48], P('head'), may hold values from -3 to 1
- d_skip: float32 [48], P('head'), may hold values from 0.5 to 1.5
- gate_gain: float32 [3072], P('head'), may hold values from 0.1 to 1.9
- w_out: bfloat16 [3072, 1536], P('head', 'seq'), may hold values from -0.109375 to 0.109375
- lengths: int32 [2, 2], replicated, may hold values from 1024 to 4096, as said below
- out_grad: bfloat16 [2, 2, 4096, 1536], P(None, None, 'seq'), may hold values from -6 to 6
Outputs:
- layer_out: bfloat16 [2, 2, 4096, 1536], P(None, None, 'seq')
- tokens_grad: bfloat16 [2, 2, 4096, 1536], P(None, None, 'seq')
- norm_gain_grad: float32 [1536], replicated
- w_z_grad: float32 [1536, 3072], P('seq', 'head')
- w_x_grad: float32 [1536, 3072], P('seq', 'head')
- w_bc_grad: float32 [1536, 256], P('seq')
- w_dt_grad: float32 [1536, 48], P('seq', 'head')
- conv_x_grad: float32 [4, 3072], P(None, 'head')
- conv_x_bias_grad: float32 [3072], P('head')
- conv_bc_grad: float32 [4, 256], replicated
- conv_bc_bias_grad: float32 [256], replicated
- dt_bias_grad: float32 [48], P('head')
- a_log_grad: float32 [48], P('head')
- d_skip_grad: float32 [48], P('head')
- gate_gain_grad: float32 [3072], P('head')
- w_out_grad: float32 [3072, 1536], P('head', 'seq')
Inputs may be any that keep to these rules, and one draw needn't show every extreme that they name: `lengths`: the first sequence of the first micro-batch uses all 4096 slots.
All inputs are finite; a program needn't handle non-finite values.
Results may differ from a plain program's by a relative error of at most 0.028.
Values may be sent and summed in bfloat16 or wider, within the bound.
A program may use at most 256 MiB of HBM per device.

v0:
```python
import math

import jax
import jax.numpy as jnp
from jax import lax
from jax.sharding import PartitionSpec as P

HEAD_DIM = 64
NST = 128
CONV = 4
MICRO = 2
DI = 3072


epsilon = 1e-05
PRECISE = lax.Precision.HIGHEST


def passed_along(value, axis, steps):
    count = lax.axis_size(axis)
    leading, last = (max(0, -steps), min(count, count - steps))
    return lax.ppermute(value, axis, [(source, source + steps) for source in range(leading, last)])


def prefix(x, axis, combine, identity):
    peers, index = (lax.axis_size(axis), lax.axis_index(axis))
    everything = jax.tree.map(
        lambda part, kind: lax.all_gather(part.astype(kind), axis), x, (jnp.bfloat16, jnp.bfloat16)
    )
    start = jax.tree.map(
        lambda part, zero: jnp.broadcast_to(jnp.asarray(zero, part.dtype), part.shape), x, identity
    )

    def hop(k, before):
        reached = k < index
        new = combine(
            before, jax.tree.map(lambda part, own: part[k].astype(own.dtype), everything, x)
        )
        return jax.tree.map(lambda a, b: jnp.where(reached, a, b), new, before)

    return lax.fori_loop(0, peers, hop, start)


def prefix_2(x, axis, join, neutral):
    count = lax.axis_size(axis)
    place = lax.axis_index(axis)
    ahead = count - 1 - place
    gathered = jax.tree.map(
        lambda a, kind: lax.all_gather(a.astype(kind), axis),
        x,
        jax.tree.map(lambda a: jnp.bfloat16 if a.dtype == jnp.float32 else a.dtype, x),
    )
    state = jax.tree.map(lambda a, e: jnp.zeros_like(a) + jnp.asarray(e, a.dtype), x, neutral)

    def one(hop, state):
        source = count - 1 - hop
        return join(
            state,
            jax.tree.map(
                lambda a, own: lax.dynamic_index_in_dim(a, source, 0, False).astype(own.dtype),
                gathered,
                x,
            ),
        )

    return lax.fori_loop(0, ahead, one, state)


def chain_combine(earlier, later):
    return (earlier[0] * later[0], later[0][:, :, None, None] * earlier[1] + later[1])


def conv_act(joined_ext, kernel, conv_bias, dt_raw, dt_bias, a_log):
    length_dev = joined_ext.shape[1] - (CONV - 1)
    conv_out = conv_bias + kernel[0] * joined_ext[:, 0:length_dev]
    for offset in range(1, CONV):
        conv_out = conv_out + kernel[offset] * joined_ext[:, offset : offset + length_dev]
    acted = jax.nn.silu(conv_out)
    inner_width = kernel.shape[1] - 2 * NST
    inner_x = acted[:, :, :inner_width].reshape(
        acted.shape[0], length_dev, inner_width // HEAD_DIM, HEAD_DIM
    )
    b_in = acted[:, :, inner_width : inner_width + NST]
    c_in = acted[:, :, inner_width + NST :]
    step_size = jax.nn.softplus(dt_raw + dt_bias)
    log_decay = -jnp.exp(a_log) * step_size
    return (inner_x, b_in, c_in, log_decay, step_size)


def local_state(inner_x, b_in, log_decay, step_size):
    cumul = jnp.cumsum(log_decay, axis=1)
    total_decay = cumul[:, -1, :]
    tail_decay = jnp.exp(total_decay[:, None, :] - cumul)
    weighted = (tail_decay * step_size)[:, :, :, None] * inner_x
    state_loc = jnp.einsum("bshp,bsn->bhpn", weighted, b_in, precision=PRECISE)
    return (jnp.exp(total_decay), state_loc)


def block_output(state_now, pieces):
    inner_blk, b_blk, c_blk, decay_blk, step_blk = pieces
    block_len = inner_blk.shape[1]
    cumul = jnp.cumsum(decay_blk, axis=1)
    positions = jnp.arange(block_len)
    causal = (positions[:, None] >= positions[None, :])[None, :, :, None]
    differ = cumul[:, :, None, :] - cumul[:, None, :, :]
    weights = jnp.where(causal, jnp.exp(jnp.where(causal, differ, 0.0)), 0.0)
    scores = jnp.einsum("btn,bsn->bts", c_blk, b_blk, precision=PRECISE)
    mixing = weights * scores[:, :, :, None]
    scaled = inner_blk * step_blk[:, :, :, None]
    local_part = jnp.einsum("btsh,bshp->bthp", mixing, scaled, precision=PRECISE)
    carried = jnp.exp(cumul)[:, :, :, None] * jnp.einsum(
        "bhpn,btn->bthp", state_now, c_blk, precision=PRECISE
    )
    total_decay = cumul[:, -1, :]
    tail_decay = jnp.exp(total_decay[:, None, :] - cumul)
    fresh = jnp.einsum(
        "bshp,bsn->bhpn",
        (tail_decay * step_blk)[:, :, :, None] * inner_blk,
        b_blk,
        precision=PRECISE,
    )
    state_next = jnp.exp(total_decay)[:, :, None, None] * state_now + fresh
    return (state_next, local_part + carried)


def split_blocks(values, block_count, block_len):
    shaped = values.reshape((values.shape[0], block_count, block_len) + values.shape[2:])
    return jnp.moveaxis(shaped, 1, 0)


def local_output(inner_x, b_in, c_in, log_decay, step_size, d_skip, entering):
    length_dev = inner_x.shape[1]
    block_len = math.gcd(length_dev, 256)
    block_count = length_dev // block_len
    pieces = (
        split_blocks(inner_x, block_count, block_len),
        split_blocks(b_in, block_count, block_len),
        split_blocks(c_in, block_count, block_len),
        split_blocks(log_decay, block_count, block_len),
        split_blocks(step_size, block_count, block_len),
    )
    _, outputs = lax.scan(jax.checkpoint(block_output), entering, pieces)
    outputs = jnp.moveaxis(outputs, 0, 1).reshape(inner_x.shape)
    return outputs + d_skip[:, None] * inner_x


def reduce_grads(big_grads, small_grads, inner_width):
    big_sum = (
        lax.psum_scatter(
            big_grads[0].astype(jnp.bfloat16), "seq", scatter_dimension=0, tiled=True
        ).astype(jnp.float32),
        lax.psum_scatter(
            big_grads[1].astype(jnp.bfloat16), "seq", scatter_dimension=0, tiled=True
        ).astype(jnp.float32),
        lax.psum_scatter(
            big_grads[2].astype(jnp.bfloat16), "seq", scatter_dimension=0, tiled=True
        ).astype(jnp.float32),
        lax.psum_scatter(
            big_grads[3].astype(jnp.bfloat16), "seq", scatter_dimension=0, tiled=True
        ).astype(jnp.float32),
        lax.psum_scatter(
            big_grads[4].astype(jnp.bfloat16), "seq", scatter_dimension=1, tiled=True
        ).astype(jnp.float32),
    )
    small_sum = lax.psum(
        (
            small_grads[0],
            small_grads[1],
            small_grads[2],
            small_grads[3],
            small_grads[4],
            small_grads[5],
            small_grads[6],
        ),
        "seq",
    )
    head_sum = (
        lax.psum(big_sum[2].astype(jnp.bfloat16), "head").astype(jnp.float32),
        lax.psum(small_sum[2][:, inner_width:].astype(jnp.bfloat16), "head").astype(jnp.float32),
        lax.psum(small_sum[3][inner_width:].astype(jnp.bfloat16), "head").astype(jnp.float32),
    )
    return (big_sum, small_sum, head_sum)


def add_trees(total_tree, extra_tree):
    return extra_tree if total_tree is None else jax.tree.map(jnp.add, total_tree, extra_tree)


def local(
    tokens,
    norm_gain,
    w_z,
    w_x,
    w_bc,
    w_dt,
    conv_x,
    conv_x_bias,
    conv_bc,
    conv_bc_bias,
    dt_bias,
    a_log,
    d_skip,
    gate_gain,
    w_out,
    lengths,
    out_grad,
):
    inner_width = w_z.shape[1]
    length_dev = tokens.shape[2]
    positions = lax.axis_index("seq") * length_dev + jnp.arange(length_dev, dtype=jnp.int32)
    kernel = jnp.concatenate([conv_x, conv_bc], axis=1)
    conv_bias = jnp.concatenate([conv_x_bias, conv_bc_bias])
    layer_outs = []
    input_grads = []
    summed = None
    for micro_index in range(MICRO):
        full_weights = (
            lax.all_gather(w_z, "seq", axis=0, tiled=True),
            lax.all_gather(w_x, "seq", axis=0, tiled=True),
            lax.all_gather(w_bc, "seq", axis=0, tiled=True),
            lax.all_gather(w_dt, "seq", axis=0, tiled=True),
            lax.all_gather(w_out, "seq", axis=1, tiled=True),
        )
        full_z, full_x, full_bc, full_dt, full_out = full_weights
        hidden = tokens[micro_index].astype(jnp.float32)
        inverse_rms = lax.rsqrt(jnp.mean(hidden * hidden, axis=-1, keepdims=True) + epsilon)
        unit_in = hidden * inverse_rms
        normed = (unit_in * norm_gain).astype(jnp.bfloat16)
        gate_z = jnp.dot(normed, full_z, preferred_element_type=jnp.float32)
        inner_pre = jnp.dot(normed, full_x, preferred_element_type=jnp.float32).astype(jnp.bfloat16)
        bc_pre = jnp.dot(normed, full_bc, preferred_element_type=jnp.float32).astype(jnp.bfloat16)
        dt_raw = jnp.dot(normed, full_dt, preferred_element_type=jnp.float32)
        joined = jnp.concatenate([inner_pre, bc_pre], axis=-1)
        edge_rows = passed_along(joined[:, length_dev - (CONV - 1) :, :], "seq", 1)
        joined_ext = jnp.concatenate([edge_rows, joined], axis=1).astype(jnp.float32)
        inner_x, b_in, c_in, log_decay, step_size = conv_act(
            joined_ext, kernel, conv_bias, dt_raw, dt_bias, a_log
        )
        decay_total, state_loc = local_state(inner_x, b_in, log_decay, step_size)
        _, entering = prefix(
            (decay_total, state_loc),
            "seq",
            chain_combine,
            (jnp.ones_like(decay_total), jnp.zeros_like(state_loc)),
        )
        ssd_out = local_output(inner_x, b_in, c_in, log_decay, step_size, d_skip, entering)
        ssd_flat = ssd_out.reshape(ssd_out.shape[0], length_dev, inner_width)
        sig_z = jax.nn.sigmoid(gate_z)
        silu_z = gate_z * sig_z
        gated_out = ssd_flat * silu_z
        square_sum = lax.psum(jnp.sum(gated_out * gated_out, axis=-1), "head")
        inverse_gate = lax.rsqrt(square_sum[:, :, None] / DI + epsilon)
        unit_gate = gated_out * inverse_gate
        gate_normed = (unit_gate * gate_gain).astype(jnp.bfloat16)
        branch = lax.psum(
            jnp.dot(gate_normed, full_out, preferred_element_type=jnp.float32).astype(jnp.bfloat16),
            "head",
        ).astype(jnp.float32)
        valid_mask = (positions[None, :] < lengths[micro_index][:, None]).astype(jnp.float32)
        layer_outs.append((hidden + valid_mask[:, :, None] * branch).astype(jnp.bfloat16))
        back_weights = (
            lax.all_gather(w_z, "seq", axis=0, tiled=True),
            lax.all_gather(w_x, "seq", axis=0, tiled=True),
            lax.all_gather(w_bc, "seq", axis=0, tiled=True),
            lax.all_gather(w_dt, "seq", axis=0, tiled=True),
            lax.all_gather(w_out, "seq", axis=1, tiled=True),
        )
        back_z, back_x, back_bc, back_dt, back_out = back_weights
        grad_out = out_grad[micro_index].astype(jnp.float32)
        grad_branch = (valid_mask[:, :, None] * grad_out).astype(jnp.bfloat16)
        grad_w_out = jnp.einsum(
            "btf,btd->fd", gate_normed, grad_branch, preferred_element_type=jnp.float32
        )
        grad_normed = jnp.einsum(
            "btd,fd->btf", grad_branch, back_out, preferred_element_type=jnp.float32
        )
        grad_gate_gain = jnp.sum(grad_normed * unit_gate, axis=(0, 1))
        grad_unit = grad_normed * gate_gain
        inner_sum = lax.psum(jnp.sum(grad_unit * unit_gate, axis=-1), "head")
        grad_gated = inverse_gate * (grad_unit - unit_gate * (inner_sum[:, :, None] / DI))
        grad_ssd = (grad_gated * silu_z).reshape(ssd_out.shape)
        grad_z = grad_gated * ssd_flat * sig_z * (1.0 + gate_z * (1.0 - sig_z))
        _, pull_output = jax.vjp(
            local_output, inner_x, b_in, c_in, log_decay, step_size, d_skip, entering
        )
        out_inner, out_bin, out_cin, out_decay, out_step, skip_grad, entering_grad = pull_output(
            grad_ssd
        )
        _, leaving = prefix_2(
            (decay_total, entering_grad),
            "seq",
            chain_combine,
            (jnp.ones_like(decay_total), jnp.zeros_like(entering_grad)),
        )
        _, pull_state = jax.vjp(local_state, inner_x, b_in, log_decay, step_size)
        state_inner, state_bin, state_decay, state_step = pull_state(
            (jnp.sum(leaving * entering, axis=(2, 3)), leaving)
        )
        _, pull_conv = jax.vjp(conv_act, joined_ext, kernel, conv_bias, dt_raw, dt_bias, a_log)
        grad_ext, grad_kernel, grad_conv_bias, grad_dt_raw, grad_dt_bias, grad_a_log = pull_conv(
            (
                out_inner + state_inner,
                out_bin + state_bin,
                out_cin,
                out_decay + state_decay,
                out_step + state_step,
            )
        )
        back_edges = passed_along(grad_ext[:, : CONV - 1, :], "seq", -1)
        own_rows = grad_ext[:, CONV - 1 :, :]
        grad_joined = jnp.concatenate(
            [
                own_rows[:, : length_dev - (CONV - 1), :],
                own_rows[:, length_dev - (CONV - 1) :, :] + back_edges,
            ],
            axis=1,
        )
        grad_low = grad_joined.astype(jnp.bfloat16)
        grad_inner_low = grad_low[:, :, :inner_width]
        grad_bc_low = grad_low[:, :, inner_width:]
        grad_z_low = grad_z.astype(jnp.bfloat16)
        grad_dt_low = grad_dt_raw.astype(jnp.bfloat16)
        grad_w_z = jnp.einsum("btd,btf->df", normed, grad_z_low, preferred_element_type=jnp.float32)
        grad_w_x = jnp.einsum(
            "btd,btf->df", normed, grad_inner_low, preferred_element_type=jnp.float32
        )
        grad_w_bc = jnp.einsum(
            "btd,btf->df", normed, grad_bc_low, preferred_element_type=jnp.float32
        )
        grad_w_dt = jnp.einsum(
            "btd,btf->df", normed, grad_dt_low, preferred_element_type=jnp.float32
        )
        grad_in_part = jnp.einsum(
            "btf,df->btd", grad_z_low, back_z, preferred_element_type=jnp.float32
        )
        grad_in_part = grad_in_part + jnp.einsum(
            "btf,df->btd", grad_inner_low, back_x, preferred_element_type=jnp.float32
        )
        grad_in_part = grad_in_part + jnp.einsum(
            "btf,df->btd", grad_bc_low, back_bc, preferred_element_type=jnp.float32
        )
        grad_in_part = grad_in_part + jnp.einsum(
            "btf,df->btd", grad_dt_low, back_dt, preferred_element_type=jnp.float32
        )
        grad_in = lax.psum(grad_in_part.astype(jnp.bfloat16), "head").astype(jnp.float32)
        grad_norm_gain = jnp.sum(grad_in * unit_in, axis=(0, 1))
        grad_scaled = grad_in * norm_gain
        grad_hidden = grad_out + inverse_rms * (
            grad_scaled - unit_in * jnp.mean(grad_scaled * unit_in, axis=-1, keepdims=True)
        )
        input_grads.append(grad_hidden.astype(jnp.bfloat16))
        big_grads = (grad_w_z, grad_w_x, grad_w_bc, grad_w_dt, grad_w_out)
        small_grads = (
            grad_norm_gain,
            grad_gate_gain,
            grad_kernel,
            grad_conv_bias,
            grad_dt_bias,
            grad_a_log,
            skip_grad,
        )
        summed = add_trees(summed, reduce_grads(big_grads, small_grads, inner_width))
    big_sum, small_sum, head_sum = summed
    return (
        jnp.stack(layer_outs),
        jnp.stack(input_grads),
        small_sum[0],
        big_sum[0],
        big_sum[1],
        head_sum[0],
        big_sum[3],
        small_sum[2][:, :inner_width],
        small_sum[3][:inner_width],
        head_sum[1],
        head_sum[2],
        small_sum[4],
        small_sum[5],
        small_sum[6],
        small_sum[1],
        big_sum[4],
    )


def solution(mesh):
    placed = (
        P(None, None, "seq", None),
        P(),
        P("seq", "head"),
        P("seq", "head"),
        P("seq", None),
        P("seq", "head"),
        P(None, "head"),
        P("head"),
        P(),
        P(),
        P("head"),
        P("head"),
        P("head"),
        P("head"),
        P("head", "seq"),
        P(),
        P(None, None, "seq", None),
    )
    return jax.shard_map(
        local,
        mesh=mesh,
        in_specs=placed,
        out_specs=(
            P(None, None, "seq", None),
            P(None, None, "seq", None),
            P(),
            P("seq", "head"),
            P("seq", "head"),
            P("seq", None),
            P("seq", "head"),
            P(None, "head"),
            P("head"),
            P(),
            P(),
            P("head"),
            P("head"),
            P("head"),
            P("head"),
            P("head", "seq"),
        ),
        check_vma=False,
    )
```

profile of v0, /device:TPU:0, one launch (start us, length us, event | category | flops | bytes accessed | tf_op | source)
XLA Modules:
  0.0 1799.6 jit_solution(11513596945182767592)
XLA Ops:
  76.3 13.4 fusion.211
  204.7 39.2 %while.155 = (s32[]{:T(128)}, f32[2,12,64,128]{3,2,1,0:T(8,128)S(1)}, f32[2,2,256,12,64]{2,4,3,1,0:T(8,128)}, f32[2,2,256,12]{2,1,3,0:T(2,128)S(1)}, f32[2,2,256...) while((s32[]{:T(128)}, ...), condition=%wide.region_20.21_spmd, body=%wide.region_17.20_spmd.sunk | while | flops 2626367488 | bytes 38443020 | solution.py:142
  261.2 39.5 %while.154 = (s32[]{:T(128)}, f32[2,12,64,128]{3,2,1,0:T(8,128)S(1)}, f32[2,2,256,12,64]{2,4,3,1,0:T(8,128)}, f32[2,2,256,12]{2,1,3,0:T(2,128)S(1)}, f32[2,2,256...) while((s32[]{:T(128)}, ...), condition=%wide.region_8.9_spmd, body=%wide.region_5.8_spmd.sunk | while | flops 2626367488 | bytes 38443020 | solution.py:142
  315.8 11.5 multiply_reduce_fusion.23
  327.4 12.1 all-reduce.28
  358.9 17.0 multiply_reduce_fusion.16
  386.0 12.0 while.156
  403.3 158.3 %while.162 = (s32[]{:T(128)}, f32[2,12,64,128]{3,2,1,0:T(8,128)}, f32[2,2,256,12,64]{2,4,3,1,0:T(8,128)}, f32[2,2,256,128]{3,2,1,0:T(8,128)}, f32[2,2,256,128]{3...) while((s32[]{:T(128)}, f32[2,12,64,128]{3,2,1,0:T(8,128)}, ...), condition=%wide.region_43.44_spmd.clone, body=%wide.region_30.43_spmd.clone.sunk | while | flops 6071185408 | bytes 71733872 | solution.py:142
  441.1 11.1 fusion.533
  520.5 11.1 fusion.533
  586.9 155.9 %while.163 = (s32[]{:T(128)}, f32[2,12,64,128]{3,2,1,0:T(8,128)}, f32[2,2,256,12,64]{2,4,3,1,0:T(8,128)}, f32[2,2,256,128]{3,2,1,0:T(8,128)}, f32[2,2,256,128]{3...) while((s32[]{:T(128)}, f32[2,12,64,128]{3,2,1,0:T(8,128)}, ...), condition=%wide.region_72.74_spmd.clone, body=%wide.region_59.73_spmd.clone.sunk | while | flops 6071185408 | bytes 78025360 | solution.py:142
  623.6 11.1 fusion.560
  701.9 11.1 fusion.560
  754.6 13.1 while.157
  776.2 13.1 while.159
  823.2 12.8 multiply_reduce_fusion.13
  1034.5 43.8 %reduce-scatter.15.cloned.1.call-done = bf16[192,768]{1,0:T(8,128)(2,1)} async-done(((bf16[1536,768]{1,0:T(8,128)(2,1)}), bf16[192,768]{1,0:T(8,128)(2,1)}) %reduce-scatter.15.cloned.1.call-update) | async-done | bytes 294928 | tf_op jit(solution)/shard_map/reduce_scatter | solution.py:149
  1078.3 46.2 %reduce-scatter.17.cloned.1.call-done = bf16[192,768]{1,0:T(8,128)(2,1)} async-done(((bf16[1536,768]{1,0:T(8,128)(2,1)}), bf16[192,768]{1,0:T(8,128)(2,1)}) %reduce-scatter.17.cloned.1.call-update) | async-done | bytes 294928 | tf_op jit(solution)/shard_map/reduce_scatter | solution.py:149
  1126.6 34.7 %reduce-scatter.31.cloned.1.call-done = bf16[192,12]{1,0:T(8,128)(2,1)} async-done(((bf16[1536,12]{1,0:T(8,128)(2,1)}), bf16[192,12]{1,0:T(8,128)(2,1)}) %reduce-scatter.31.cloned.1.call-update) | async-done | bytes 4624
  1162.1 36.5 %reduce-scatter.33.cloned.1.call-done = bf16[192,12]{1,0:T(8,128)(2,1)} async-done(((bf16[1536,12]{1,0:T(8,128)(2,1)}), bf16[192,12]{1,0:T(8,128)(2,1)}) %reduce-scatter.33.cloned.1.call-update) | async-done | bytes 4624
  1200.1 44.2 %reduce-scatter.19.cloned.1.call-done = bf16[192,768]{1,0:T(8,128)(2,1)} async-done(((bf16[1536,768]{1,0:T(8,128)(2,1)}), bf16[192,768]{1,0:T(8,128)(2,1)}) %reduce-scatter.19.cloned.1.call-update) | async-done | bytes 294928 | tf_op jit(solution)/shard_map/reduce_scatter | solution.py:152
  1244.3 46.1 %reduce-scatter.21.cloned.1.call-done = bf16[192,768]{1,0:T(8,128)(2,1)} async-done(((bf16[1536,768]{1,0:T(8,128)(2,1)}), bf16[192,768]{1,0:T(8,128)(2,1)}) %reduce-scatter.21.cloned.1.call-update) | async-done | bytes 294928 | tf_op jit(solution)/shard_map/reduce_scatter | solution.py:152
  1292.3 437.6 %all-reduce.33.cloned.1.call-done = (bf16[2,512,1536]{2,1,0:T(8,128)(2,1)}, bf16[2,512,1536]{2,1,0:T(8,128)(2,1)}, bf16[2,512,1536]{2,1,0:T(8,128)(2,1)}, bf16[2...) async-done(((bf16[2,512,1536]{2,1,0:T(8,128)(2,1)}, bf16[2,512,1536]{2,1,0:T(8,128)(2,1)}, bf16[2,512,1536]{2,1,0:T(8,128)(2,1)}, ...) | async-done | bytes 12779536 | tf_op jit(solution)/shard_map/psum | solution.py:255
  1737.7 25.1 %all-reduce.26 = (f32[1536]{0:T(1024)}, f32[4,1024]{1,0:T(4,128)S(1)}, f32[4,1024]{1,0:T(4,128)S(1)}, f32[1024]{0:T(1024)S(1)}, f32[1024]{0:T(1024)S(1)}, /*inde...) all-reduce(f32[1536]{0:T(1024)S(1)} %add.604, ...), channel_id=1, replica_groups=mesh['seq'=8,'head'=4] {'seq'}, use_global_device_ids=true, to_apply=%region_83.85 | all-reduce | flops 12580 | bytes 100640 | tf_op jit(solution)/shard_map/psum | solution.py:165
  (1134 shorter events, 982.8 us)
Async XLA Ops:
  7.2 50.7 %all-gather.15.cloned.1.call-start = ((), (), s32[]{:S(2)}) async-start(), calls=%async_computation.10 | async-start | bytes 2654208 | tf_op jit(solution)/shard_map/all_gather | solution.py:219
  7.9 137.7 %all-gather.19.cloned.1.call-start = ((), (), s32[]{:S(2)}) async-start(), calls=%async_computation.12 | async-start | bytes 2654208 | tf_op jit(solution)/shard_map/all_gather | solution.py:222
  8.7 144.2 %all-gather.17.cloned.1.call-start = ((), (), s32[]{:S(2)}) async-start(), calls=%async_computation.11 | async-start | bytes 2654208 | tf_op jit(solution)/shard_map/all_gather | solution.py:218
  9.4 171.2 %all-gather.21.cloned.1.call-start = ((), (), s32[]{:S(2)}) async-start(), calls=%async_computation.21 | async-start | bytes 3538944 | tf_op jit(solution)/shard_map/all_gather | solution.py:28
  23.9 292.0 %copy-start.110 = (f32[2,512]{1,0:T(2,128)}, f32[2,512]{1,0:T(2,128)S(1)}, u32[]{:S(2)}) copy-start(f32[2,512]{1,0:T(2,128)S(1)} %get-tuple-element.1977) | copy-start | bytes 12292
  63.3 9.6 collective-permute-start
  70.2 5.4 collective-permute-start.1
  101.1 89.5 %all-gather.23.cloned.1.call-start = ((), (), s32[]{:S(2)}) async-start(), calls=%async_computation.22 | async-start | bytes 3538944 | tf_op jit(solution)/shard_map/all_gather | solution.py:28
  123.3 631.2 %all-gather.25.cloned.1.call-start = ((), (), s32[]{:S(2)}) async-start(), calls=%async_computation.23 | async-start | bytes 3538944 | tf_op jit(solution)/shard_map/all_gather | solution.py:49
  145.6 193.9 %copy-start.136 = (f32[2,512]{1,0:T(2,128)}, f32[2,512]{1,0:T(2,128)S(1)}, u32[]{:S(2)}) copy-start(f32[2,512]{1,0:T(2,128)S(1)} %get-tuple-element.1961) | copy-start | bytes 12292
  563.7 212.4 %all-gather.27.cloned.1.call-start = ((), (), s32[]{:S(2)}) async-start(), calls=%async_computation.24 | async-start | bytes 3538944 | tf_op jit(solution)/shard_map/all_gather | solution.py:49
  744.9 277.4 %reduce-scatter.23.cloned.1.call-start = ((), (), s32[]{:S(2)}) async-start(), calls=%async_computation.17 | async-start | bytes 884736 | tf_op jit(solution)/shard_map/reduce_scatter | solution.py:155
  852.2 9.4 collective-permute-start.2
  867.3 154.9 %reduce-scatter.25.cloned.1.call-start = ((), (), s32[]{:S(2)}) async-start(), calls=%async_computation.18 | async-start | bytes 884736 | tf_op jit(solution)/shard_map/reduce_scatter | solution.py:155
  868.5 11.7 collective-permute-start.3
  886.1 137.3 %reduce-scatter.27.cloned.1.call-start = ((), (), s32[]{:S(2)}) async-start(), calls=%async_computation.19 | async-start | bytes 2654208 | tf_op jit(solution)/shard_map/reduce_scatter | solution.py:161
  894.2 138.3 %reduce-scatter.29.cloned.1.call-start = ((), (), s32[]{:S(2)}) async-start(), calls=%async_computation.20 | async-start | bytes 2654208 | tf_op jit(solution)/shard_map/reduce_scatter | solution.py:161
  900.7 177.5 %reduce-scatter.15.cloned.1.call-start = ((), (), s32[]{:S(2)}) async-start(), calls=%async_computation.13 | async-start | bytes 2654208 | tf_op jit(solution)/shard_map/reduce_scatter | solution.py:149
  907.6 216.9 %reduce-scatter.17.cloned.1.call-start = ((), (), s32[]{:S(2)}) async-start(), calls=%async_computation.14 | async-start | bytes 2654208 | tf_op jit(solution)/shard_map/reduce_scatter | solution.py:149
  916.3 245.0 %reduce-scatter.31.cloned.1.call-start = ((), (), s32[]{:S(2)}) async-start(), calls=%async_computation.25 | async-start | bytes 442368
  960.2 238.4 %reduce-scatter.33.cloned.1.call-start = ((), (), s32[]{:S(2)}) async-start(), calls=%async_computation.26 | async-start | bytes 442368
  964.4 279.9 %reduce-scatter.19.cloned.1.call-start = ((), (), s32[]{:S(2)}) async-start(), calls=%async_computation.15 | async-start | bytes 2654208 | tf_op jit(solution)/shard_map/reduce_scatter | solution.py:152
  970.9 319.5 %reduce-scatter.21.cloned.1.call-start = ((), (), s32[]{:S(2)}) async-start(), calls=%async_computation.16 | async-start | bytes 2654208 | tf_op jit(solution)/shard_map/reduce_scatter | solution.py:152
  996.2 733.7 %all-reduce.33.cloned.1.call-start = ((), (), s32[]{:S(2)}) async-start(), calls=%async_computation.27 | async-start | bytes 25559040 | tf_op jit(solution)/shard_map/psum | solution.py:255
  (197 other events, 2646.3 us)
Sparse Core Ops, SparseCore 0:
  9.9 31.7 all-gather.14
  43.6 29.1 all-gather.18
  74.6 29.0 all-gather.16
  105.5 32.3 all-gather.20
  139.5 32.3 all-gather.22
  563.8 31.0 all-gather.24
  745.0 31.1 all-gather.26
  867.5 34.8 reduce-scatter.22
  905.5 34.9 reduce-scatter.24
  943.7 42.5 reduce-scatter.26
  990.0 42.4 reduce-scatter.28
  1035.7 42.4 reduce-scatter.14
  1082.0 42.4 reduce-scatter.16
  1127.4 33.8 reduce-scatter.30
  1164.7 33.8 reduce-scatter.32
  1201.8 42.4 reduce-scatter.18
  1247.9 42.4 reduce-scatter.20
  1294.0 435.8 all-reduce.32
where the time goes:
time: 1810 us; the launch traced here: 1800 us
  waiting for transfers between devices  709 us (39%)
  matrix products  420 us (23%)
  other arithmetic  287 us (16%)
  local copies, waits for them, and re-layouts  259 us (14%)
  blocking collectives  94.1 us (5%)
    psum x1, waiting for transfers between devices, local(): lax.psum(jnp.dot(gate_normed, full_out, preferred_element_type=jnp.float3...  438 us
    dot_general x12, matrix products, block_output(): jnp.einsum('btsh,bshp->bthp', mixing, scaled, precision=PRECISE)  114 us
    reduce_scatter x2, waiting for transfers between devices, reduce_grads(): lax.psum_scatter(big_grads[1].astype(jnp.bfloat16), 'seq', scatter_dimens...  90.3 us
    reduce_scatter x2, waiting for transfers between devices, reduce_grads(): lax.psum_scatter(big_grads[0].astype(jnp.bfloat16), 'seq', scatter_dimens...  90 us
    unnamed x20, waiting for transfers between devices  73.5 us
    another operation x63, other arithmetic  61.1 us
    dot_general x16, matrix products, block_output(): jnp.einsum('bshp,bsn->bhpn', (tail_decay * step_blk)[:, :, :, None] * inn...  51.7 us
    dot_general x6, matrix products, local_state(): state_loc = jnp.einsum('bshp,bsn->bhpn', weighted, b_in, precision=PRECISE)  37.7 us
  transfers between devices with their start and end apart: 22, of which 9 were waited for; matrix products, arithmetic and copies ran while one was open for 28% of the time, Pallas kernels for 0%

commit v1 on v0

v1 whole, which is shorter than its diff:
```python
import functools

import jax
import jax.numpy as jnp
from jax import lax
from jax.experimental import pallas as pl
from jax.experimental.pallas import tpu as pltpu
from jax.sharding import PartitionSpec as P

HEAD_DIM = 64
NST = 128
CONV = 4
CHUNK = 128
LANES = 128
EDGE = 8
GROUPS = 4

epsilon = 1e-05
f32 = jnp.float32
bf16 = jnp.bfloat16

NN = (((1,), (0,)), ((), ()))
NT = (((1,), (1,)), ((), ()))
TN = (((0,), (0,)), ((), ()))


def mm(a, b, dims=NN):
    return lax.dot_general(a, b, dims, preferred_element_type=f32)


def mm_split(a, b, dims=NN):
    high = a.astype(bf16)
    low = (a - high.astype(f32)).astype(bf16)
    return mm(high, b, dims) + mm(low, b, dims)


def mm_split_right(a, b, dims=NN):
    high = b.astype(bf16)
    rest = b - high.astype(f32)
    mid = rest.astype(bf16)
    low = (rest - mid.astype(f32)).astype(bf16)
    return mm(a, high, dims) + (mm(a, mid, dims) + mm(a, low, dims))


def sigmoid(v):
    return 1.0 / (1.0 + jnp.exp(-v))


def softplus(v):
    return jnp.maximum(v, 0.0) + jnp.log1p(jnp.exp(-jnp.abs(v)))


def iotas(rows, cols):
    return (
        lax.broadcasted_iota(jnp.int32, (rows, cols), 0),
        lax.broadcasted_iota(jnp.int32, (rows, cols), 1),
    )


def lower_ones():
    row, col = iotas(CHUNK, CHUNK)
    return (row >= col).astype(bf16)


def conv_rows(ext, taps, rows):
    total = taps[CONV : CONV + 1, :] + taps[0:1, :] * ext[EDGE - 3 : EDGE - 3 + rows, :]
    for k in range(1, CONV):
        total = total + taps[k : k + 1, :] * ext[EDGE - 3 + k : EDGE - 3 + k + rows, :]
    return total


def chunk_decays(dt_raw, heads_ref):
    step = softplus(dt_raw + heads_ref[0:1, :])
    log_decay = -jnp.exp(heads_ref[1:2, :]) * step
    cumul = mm_split_right(lower_ones(), log_decay)
    return step, cumul


def pair_weights(cumul, cumul_t, head, causal):
    differ = cumul[:, head : head + 1] - cumul_t[head : head + 1, :]
    return jnp.exp(jnp.where(causal, differ, -1e30))


def block_diag(pair, low_lanes):
    zero = jnp.zeros_like(pair)
    return jnp.concatenate(
        [jnp.where(low_lanes, pair, zero), jnp.where(low_lanes, zero, pair)], axis=0
    )


def project_kernel(
    tok_ref,
    halo_ref,
    gain_ref,
    w_ref,
    taps_ref,
    heads_ref,
    spread_ref,
    normed_ref,
    proj_ref,
    dt_ref,
    acted_ref,
    local_ref,
    cumul_ref,
    states_ref,
    total_ref,
    edge_ref,
    joined,
    state,
):
    rows = tok_ref.shape[1]
    width = spread_ref.shape[1]
    wide = width + 2 * NST
    tile = 384

    def norm(v):
        v = v.astype(f32)
        inverse = lax.rsqrt(jnp.mean(v * v, axis=-1, keepdims=True) + epsilon)
        return (v * inverse * gain_ref[...]).astype(bf16)

    edge = mm(norm(halo_ref[0]), w_ref[:, width : 2 * width + 2 * NST])
    edge = edge.astype(bf16).astype(f32)[EDGE:, :]
    joined[0:EDGE, :] = edge
    edge_ref[0] = edge
    normed_ref[0] = norm(tok_ref[0])
    for start in range(0, 2 * width, tile):
        part = mm(normed_ref[0], w_ref[:, start : start + tile]).astype(bf16)
        proj_ref[0, :, start : start + tile] = part
        if start >= width:
            joined[EDGE:, start - width : start - width + tile] = part.astype(f32)
    last = mm(normed_ref[0], w_ref[:, 2 * width :])
    part = last[:, : 2 * NST].astype(bf16)
    proj_ref[0, :, 2 * width :] = part
    joined[EDGE:, width:] = part.astype(f32)
    dt_ref[0] = last[:, 2 * NST :]

    row, col = iotas(CHUNK, CHUNK)
    causal = row >= col
    low_lanes = col < HEAD_DIM
    state[...] = jnp.zeros_like(state)

    def chunk(index, base):
        start = pl.multiple_of(index * CHUNK, CHUNK)
        here = pl.ds(start, CHUNK)
        conv = conv_rows(joined[pl.ds(start, CHUNK + EDGE), :], taps_ref, CHUNK)
        acted = conv * sigmoid(conv)
        acted_low = acted.astype(bf16)
        acted_ref[0, here, :] = acted_low
        b_low = acted_low[:, width : width + NST]
        c_low = acted_low[:, width + NST :]
        step, cumul = chunk_decays(dt_ref[0, here, :], heads_ref)
        cumul_t = cumul.T
        final = cumul[CHUNK - 1 :, :]
        cumul_ref[0, here, :] = cumul + base
        scaled = mm_split(step, spread_ref[...]) * acted[:, :width]
        scaled_low = scaled.astype(bf16)
        scores = mm(c_low, b_low, NT)
        states_ref[0, pl.ds(index, 1)] = state[...].astype(bf16)[None]
        carried = mm_split(jnp.exp(cumul), spread_ref[...]) * mm(c_low, state[...].astype(bf16))
        for pair in range(width // LANES):
            lanes = slice(pair * LANES, (pair + 1) * LANES)
            mixing = [
                (pair_weights(cumul, cumul_t, 2 * pair + k, causal) * scores).astype(bf16)
                for k in (0, 1)
            ]
            here_out = mm(
                jnp.concatenate(mixing, axis=1), block_diag(scaled_low[:, lanes], low_lanes)
            )
            local_ref[0, here, lanes] = (here_out + carried[:, lanes]).astype(bf16)
        tail = mm_split(jnp.exp(final - cumul), spread_ref[...])
        fresh = mm(b_low, (scaled * tail).astype(bf16), TN)
        keep = mm_split(jnp.broadcast_to(jnp.exp(final), (EDGE, LANES)), spread_ref[...])[0:1, :]
        state[...] = keep * state[...] + fresh
        return base + final

    base = lax.fori_loop(0, rows // CHUNK, chunk, jnp.zeros((1, LANES), f32))
    total_ref[0, 0:NST, :] = state[...].astype(bf16)
    decay = mm_split(jnp.broadcast_to(jnp.exp(base), (2 * EDGE, LANES)), spread_ref[...])
    high = decay.astype(bf16)
    first = lax.broadcasted_iota(jnp.int32, decay.shape, 0) == 0
    total_ref[0, NST:, :] = jnp.where(first, high.astype(f32), decay - high.astype(f32)).astype(bf16)


def gate_kernel(
    acted_ref,
    local_ref,
    cumul_ref,
    z_ref,
    enter_ref,
    grad_ref,
    w_out_ref,
    spread_ref,
    chan_ref,
    ssd_ref,
    gn_ref,
    sums_ref,
):
    rows = acted_ref.shape[1]
    width = spread_ref.shape[1]
    gn_ref[0] = mm(grad_ref[0], w_out_ref[...], NT).astype(bf16)

    def chunk(index, carry):
        here = pl.ds(pl.multiple_of(index * CHUNK, CHUNK), CHUNK)
        c_low = acted_ref[0, here, width + NST :]
        carried = mm_split(jnp.exp(cumul_ref[0, here, :]), spread_ref[...]) * mm(
            c_low, enter_ref[0]
        )
        ssd = (
            local_ref[0, here, :].astype(f32)
            + carried
            + chan_ref[1:2, :] * acted_ref[0, here, :width].astype(f32)
        )
        ssd_low = ssd.astype(bf16)
        ssd_ref[0, here, :] = ssd_low
        gate = z_ref[0, here, :].astype(f32)
        gated = ssd_low.astype(f32) * (gate * sigmoid(gate))
        square = jnp.sum(gated * gated, axis=-1, keepdims=True)
        inner = jnp.sum(
            gn_ref[0, here, :].astype(f32) * chan_ref[0:1, :] * gated, axis=-1, keepdims=True
        )
        _, col = iotas(CHUNK, LANES)
        both = jnp.where(col == 0, square, jnp.where(col == 1, inner, 0.0))
        sums_ref[0, :, here] = both.T[0:EDGE, :]
        return carry

    lax.fori_loop(0, rows // CHUNK, chunk, 0)


def mixer_kernel(
    sums_ref,
    ssd_ref,
    z_ref,
    gn_ref,
    acted_ref,
    dt_ref,
    cumul_ref,
    states_ref,
    enter_ref,
    w_out_ref,
    heads_ref,
    spread_ref,
    chan_ref,
    gnorm_ref,
    branch_ref,
    gz_ref,
    dx_ref,
    dbc_ref,
    ddt_ref,
    dld_ref,
    total_ref,
    cols_ref,
    grad_state,
    *,
    inner_total,
):
    rows = acted_ref.shape[1]
    width = spread_ref.shape[1]
    chunks = rows // CHUNK
    row, col = iotas(CHUNK, CHUNK)
    causal = row >= col
    low_lanes = col < HEAD_DIM
    grad_state[...] = jnp.zeros_like(grad_state)
    cols_ref[0] = jnp.zeros_like(cols_ref[0])
    spread = spread_ref[...]

    def chunk(turn, carry):
        index = chunks - 1 - turn
        start = pl.multiple_of(index * CHUNK, CHUNK)
        here = pl.ds(start, CHUNK)
        sums = jnp.concatenate(
            [sums_ref[0, :, here], jnp.zeros((CHUNK - EDGE, CHUNK), f32)], axis=0
        ).T
        inverse = lax.rsqrt(sums[:, 0:1] / inner_total + epsilon)
        inner_mean = inverse * sums[:, 1:2] / inner_total
        gate = z_ref[0, here, :].astype(f32)
        sig = sigmoid(gate)
        silu = gate * sig
        ssd = ssd_ref[0, here, :].astype(f32)
        unit = ssd * silu * inverse
        gnorm_ref[0, here, :] = (unit * chan_ref[0:1, :]).astype(bf16)
        gn = gn_ref[0, here, :].astype(f32)
        grad_gated = inverse * (gn * chan_ref[0:1, :] - unit * inner_mean)
        grad_ssd = grad_gated * silu
        gz_ref[0, here, :] = (grad_gated * ssd * sig * (1.0 + gate * (1.0 - sig))).astype(bf16)
        x_low = acted_ref[0, here, :width]
        x = x_low.astype(f32)
        b_low = acted_ref[0, here, width : width + NST]
        c_low = acted_ref[0, here, width + NST :]
        cols_ref[0, 0:1, :] += jnp.sum(gn * unit, axis=0, keepdims=True)
        cols_ref[0, 1:2, :] += jnp.sum(x * grad_ssd, axis=0, keepdims=True)

        step, cumul = chunk_decays(dt_ref[0, here, :], heads_ref)
        cumul_t = cumul.T
        final = cumul[CHUNK - 1 :, :]
        before = cumul_ref[0, here, :][0:1, :] - cumul[0:1, :]
        step_wide = mm_split(step, spread)
        scaled = step_wide * x
        scaled_low = scaled.astype(bf16)
        dy_low = grad_ssd.astype(bf16)
        dy = dy_low.astype(f32)
        grown = mm_split(jnp.exp(cumul), spread)
        tail = mm_split(jnp.exp(final - cumul), spread)
        keeps = mm_split(
            jnp.concatenate(
                [
                    jnp.broadcast_to(jnp.exp(final), (EDGE, LANES)),
                    jnp.broadcast_to(jnp.exp(before), (EDGE, LANES)),
                ],
                axis=0,
            ),
            spread,
        )
        keep = keeps[0:1, :]
        state = (
            states_ref[0, pl.ds(index, 1)][0].astype(f32)
            + keeps[EDGE : EDGE + 1, :] * enter_ref[0].astype(f32)
        )
        state_low = state.astype(bf16)
        later = grad_state[...]
        later_low = later.astype(bf16)
        scores = mm(c_low, b_low, NT)
        carried = grown * mm(c_low, state_low)
        tail_grad = tail * mm(b_low, later_low)
        score_grad = jnp.zeros((CHUNK, CHUNK), f32)
        rising = []
        falling = []
        for pair in range(width // LANES):
            lanes = slice(pair * LANES, (pair + 1) * LANES)
            decays = [pair_weights(cumul, cumul_t, 2 * pair + k, causal) for k in (0, 1)]
            mixing = [(d * scores).astype(bf16) for d in decays]
            scaled_two = block_diag(scaled_low[:, lanes], low_lanes)
            dy_two = block_diag(dy_low[:, lanes], low_lanes)
            out = mm(jnp.concatenate(mixing, axis=1), scaled_two)
            mixing_grad = mm(dy_low[:, lanes], scaled_two, NT)
            own_grad = mm(jnp.concatenate(mixing, axis=0), dy_two, TN)
            score_grad = (
                score_grad
                + mixing_grad[:, :CHUNK] * decays[0]
                + mixing_grad[:, CHUNK:] * decays[1]
            )
            scaled_back = scaled_low[:, lanes].astype(f32)
            rising.append(
                dy[:, lanes] * (out + carried[:, lanes]) - scaled_back * own_grad
            )
            falling.append(own_grad)
        own_all = jnp.concatenate(falling, axis=1)
        scaled_grad = own_all + tail_grad
        rise = mm_split(jnp.concatenate(rising, axis=1), spread, NT)
        fall = mm_split(scaled * tail_grad, spread, NT)
        dx_ref[0, here, :] = (step_wide * scaled_grad + chan_ref[1:2, :] * grad_ssd).astype(bf16)
        ddt_ref[0, here, :] = mm_split(x * scaled_grad, spread, NT)
        at_end = mm_split(
            jnp.broadcast_to(jnp.sum(later * state * keep, axis=0, keepdims=True), (EDGE, width)),
            spread,
            NT,
        )[0:1, :]
        upper = (row <= col).astype(bf16)
        under = (row > col).astype(bf16)
        dld_ref[0, here, :] = mm_split_right(upper, rise) + mm_split_right(under, fall) + at_end
        score_low = score_grad.astype(bf16)
        dy_grown = (dy * grown).astype(bf16)
        db = mm(score_low, c_low, TN) + mm((scaled * tail).astype(bf16), later_low, NT)
        dc = mm(score_low, b_low) + mm(dy_grown, state_low, NT)
        dbc_ref[0, here, 0:NST] = db
        dbc_ref[0, here, NST:] = dc
        grad_state[...] = keep * later + mm(c_low, dy_grown, TN)
        return carry

    lax.fori_loop(0, chunks, chunk, 0)
    total_ref[0] = grad_state[...].astype(bf16)
    branch_ref[0] = mm(gnorm_ref[0], w_out_ref[...]).astype(bf16)


def conv_kernel(
    proj_ref,
    edge_ref,
    acted_ref,
    dx_ref,
    dbc_ref,
    ddt_ref,
    dld_ref,
    dt_ref,
    cumul_ref,
    enter_ref,
    leave_ref,
    taps_ref,
    heads_ref,
    spread_ref,
    gj_ref,
    gdt_ref,
    first_ref,
    tapsum_ref,
    headsum_ref,
    joined,
    grads,
):
    rows = acted_ref.shape[1]
    width = spread_ref.shape[1]
    chunks = rows // CHUNK
    spread = spread_ref[...]
    joined[0:EDGE, :] = edge_ref[0]
    joined[EDGE:, :] = proj_ref[0, :, width:].astype(f32)
    tapsum_ref[0] = jnp.zeros_like(tapsum_ref[0])
    headsum_ref[0] = jnp.zeros_like(headsum_ref[0])
    grads[rows:, :] = jnp.zeros((EDGE, width + 2 * NST), f32)
    leave = leave_ref[0]
    enter = enter_ref[0]
    final = cumul_ref[0, rows - EDGE :, :][EDGE - 1 :, :]
    held = jnp.sum(leave.astype(f32) * enter.astype(f32), axis=0, keepdims=True)
    at_end = mm_split(jnp.broadcast_to(held, (EDGE, width)), spread, NT)[0:1, :] * jnp.exp(final)
    row, col = iotas(CHUNK, CHUNK)
    under = (row > col).astype(bf16)
    rate = jnp.exp(heads_ref[1:2, :])

    def chunk(index, passed):
        start = pl.multiple_of(index * CHUNK, CHUNK)
        here = pl.ds(start, CHUNK)
        conv_ext = joined[pl.ds(start, CHUNK + EDGE), :]
        conv = conv_rows(conv_ext, taps_ref, CHUNK)
        sig = sigmoid(conv)
        slope = sig * (1.0 + conv * (1.0 - sig))
        x = acted_ref[0, here, :width].astype(f32)
        b_low = acted_ref[0, here, width : width + NST]
        raw = dt_ref[0, here, :] + heads_ref[0:1, :]
        step = softplus(raw)
        step_wide = mm_split(step, spread)
        tail = mm_split(jnp.exp(final - cumul_ref[0, here, :]), spread)
        tail_grad = tail * mm(b_low, leave)
        scaled = step_wide * x
        dx = dx_ref[0, here, :].astype(f32) + step_wide * tail_grad
        db = dbc_ref[0, here, 0:NST] + mm((scaled * tail).astype(bf16), leave, NT)
        dc = dbc_ref[0, here, NST:]
        moved = mm_split(x * tail_grad, spread, NT)
        fall = moved * step
        dstep = ddt_ref[0, here, :] + moved
        dld = dld_ref[0, here, :] + mm_split_right(under, fall) + passed + at_end
        gdt = (dstep - rate * dld) * sigmoid(raw)
        gdt_ref[0, here, :] = gdt.astype(bf16)
        headsum_ref[0, 0:1, :] += jnp.sum(gdt, axis=0, keepdims=True)
        headsum_ref[0, 1:2, :] += -rate * jnp.sum(step * dld, axis=0, keepdims=True)
        grad = jnp.concatenate([dx, db, dc], axis=1) * slope
        grads[here, :] = grad
        for k in range(CONV):
            tapsum_ref[0, k : k + 1, :] += jnp.sum(
                grad * conv_ext[EDGE - 3 + k : EDGE - 3 + k + CHUNK, :], axis=0, keepdims=True
            )
        tapsum_ref[0, CONV : CONV + 1, :] += jnp.sum(grad, axis=0, keepdims=True)
        return passed + jnp.sum(fall, axis=0, keepdims=True)

    lax.fori_loop(0, chunks, chunk, jnp.zeros((1, LANES), f32))
    first_ref[0] = grads[0:EDGE, :]

    def back(index, carry):
        start = pl.multiple_of(index * CHUNK, CHUNK)
        ext = grads[pl.ds(start, CHUNK + EDGE), :]
        total = taps_ref[CONV - 1 : CONV, :] * ext[0:CHUNK, :]
        for k in range(CONV - 1):
            total = total + taps_ref[k : k + 1, :] * ext[3 - k : 3 - k + CHUNK, :]
        gj_ref[0, pl.ds(start, CHUNK), :] = total.astype(bf16)
        return carry

    lax.fori_loop(0, chunks, back, 0)


def input_kernel(gz_ref, gj_ref, gdt_ref, next_ref, taps_ref, w_ref, fixed_ref, out_ref):
    rows = gz_ref.shape[1]
    width = gz_ref.shape[2]
    wide = gj_ref.shape[2]
    ext = jnp.concatenate([jnp.zeros((2 * EDGE, wide), f32), next_ref[0]], axis=0)
    extra = jnp.zeros((2 * EDGE, wide), f32)
    for k in range(CONV - 1):
        extra = extra + taps_ref[k : k + 1, :] * ext[3 - k : 3 - k + 2 * EDGE, :]
    fixed_ref[0] = gj_ref[0]
    tail = slice(rows - 2 * EDGE, rows)
    fixed_ref[0, tail, :] = (gj_ref[0, tail, :].astype(f32) + extra).astype(bf16)
    tile = 384
    for start in range(0, out_ref.shape[2], tile):
        part = slice(start, start + tile)
        total = mm(gz_ref[0], w_ref[part, :width], NT)
        total = total + mm(fixed_ref[0], w_ref[part, width : width + wide], NT)
        total = total + mm(gdt_ref[0], w_ref[part, width + wide :], NT)
        out_ref[0, :, part] = total.astype(bf16)


def per_sequence(shape):
    zeros = (0,) * (len(shape) - 1)
    return pl.BlockSpec((1,) + tuple(shape[1:]), lambda i: (i,) + zeros)


def whole(shape):
    zeros = (0,) * len(shape)
    return pl.BlockSpec(tuple(shape), lambda i: zeros, pipeline_mode=pl.Buffered(1))


def run(body, name, count, streamed, fixed, outs, scratch, flops, order=None):
    operands = list(streamed) + list(fixed)
    moved = sum(a.size * a.dtype.itemsize for a in operands)
    moved += sum(o.size * o.dtype.itemsize for o in outs)
    return pl.pallas_call(
        body,
        name=name,
        grid=(count,),
        in_specs=[per_sequence(a.shape) for a in streamed] + [whole(a.shape) for a in fixed],
        out_specs=[per_sequence(o.shape) for o in outs],
        out_shape=outs,
        scratch_shapes=scratch,
        compiler_params=pltpu.CompilerParams(vmem_limit_bytes=60 * 1024 * 1024),
        cost_estimate=pl.CostEstimate(flops=flops, bytes_accessed=moved, transcendentals=0),
    )(*operands)


def spec(*shape, dtype=f32):
    return jax.ShapeDtypeStruct(shape, dtype)


def exchange(total, axis, forward):
    size = lax.axis_size(axis)
    place = lax.axis_index(axis)
    state = total[:, :NST].astype(f32)
    decay = jnp.sum(total[:, NST : NST + 2].astype(f32), axis=1, keepdims=True)
    met = jnp.zeros_like(state)
    met_decay = jnp.ones_like(decay)
    payload = total
    bit = 1
    while bit < size:
        got = lax.ppermute(payload, axis, [(i, i ^ bit) for i in range(size)])
        other = got[:, :NST].astype(f32)
        other_decay = jnp.sum(got[:, NST : NST + 2].astype(f32), axis=1, keepdims=True)
        upper = (place & bit) != 0
        earlier = upper if forward else jnp.logical_not(upper)
        met = jnp.where(earlier, met_decay * other + met, met)
        met_decay = jnp.where(earlier, met_decay * other_decay, met_decay)
        bit *= 2
        if bit < size:
            state = jnp.where(earlier, decay * other + state, other_decay * state + other)
            decay = decay * other_decay
            high = decay.astype(bf16)
            low = (decay - high.astype(f32)).astype(bf16)
            payload = jnp.concatenate(
                [state.astype(bf16), high, low, jnp.zeros_like(total[:, NST + 2 :])], axis=1
            )
    return met.astype(bf16)


def local(
    tokens,
    norm_gain,
    w_z,
    w_x,
    w_bc,
    w_dt,
    conv_x,
    conv_x_bias,
    conv_bc,
    conv_bc_bias,
    dt_bias,
    a_log,
    d_skip,
    gate_gain,
    w_out,
    lengths,
    out_grad,
):
    micro, seqs, rows, model = tokens.shape
    batch = micro * seqs
    width = w_z.shape[1]
    heads = width // HEAD_DIM
    wide = width + 2 * NST
    inner_total = width * lax.axis_size("head")
    per = batch // GROUPS
    flat = tokens.reshape(batch, rows, model)
    flat_grad = out_grad.reshape(batch, rows, model)

    seq_size = lax.axis_size("seq")
    halo = lax.ppermute(
        flat[:, rows - 2 * EDGE :, :], "seq", [(i, i + 1) for i in range(seq_size - 1)]
    )
    keep_rows = jnp.arange(2 * EDGE) >= 2 * EDGE - (CONV - 1)
    halo = jnp.where(keep_rows[None, :, None], halo, jnp.zeros_like(halo))

    w_shard = jnp.concatenate(
        [w_z, w_x, w_bc, w_dt, jnp.zeros((w_dt.shape[0], LANES - heads), bf16)], axis=1
    )
    w_all = lax.all_gather(w_shard, "seq", axis=0, tiled=True)
    w_back = lax.all_gather(w_out, "seq", axis=1, tiled=True)

    positions = lax.axis_index("seq") * rows + jnp.arange(rows, dtype=jnp.int32)
    valid = positions[None, :] < lengths.reshape(batch)[:, None]
    grad_branch = jnp.where(valid[:, :, None], flat_grad, jnp.zeros_like(flat_grad))

    taps = jnp.concatenate(
        [
            jnp.concatenate([conv_x, conv_bc], axis=1),
            jnp.concatenate([conv_x_bias, conv_bc_bias])[None],
            jnp.zeros((EDGE - CONV - 1, wide), f32),
        ],
        axis=0,
    )
    pad = LANES - heads
    head_rows = jnp.concatenate(
        [
            jnp.concatenate([dt_bias, jnp.full((pad,), -1e4, f32)])[None],
            jnp.concatenate([a_log, jnp.zeros((pad,), f32)])[None],
            jnp.zeros((EDGE - 2, LANES), f32),
        ],
        axis=0,
    )
    spread = (
        jnp.arange(LANES)[:, None] == (jnp.arange(width) // HEAD_DIM)[None, :]
    ).astype(bf16)
    chan = jnp.concatenate(
        [
            gate_gain[None],
            jnp.repeat(d_skip, HEAD_DIM)[None],
            jnp.zeros((EDGE - 2, width), f32),
        ],
        axis=0,
    )
    chunks = rows // CHUNK

    first = []
    for g in range(GROUPS):
        part = slice(g * per, (g + 1) * per)
        first.append(
            run(
                project_kernel,
                "project",
                per,
                [flat[part], halo[part]],
                [norm_gain[None], w_all, taps, head_rows, spread],
                [
                    spec(per, rows, model, dtype=bf16),
                    spec(per, rows, 2 * width + 2 * NST, dtype=bf16),
                    spec(per, rows, LANES),
                    spec(per, rows, wide, dtype=bf16),
                    spec(per, rows, width, dtype=bf16),
                    spec(per, rows, LANES),
                    spec(per, chunks, NST, width, dtype=bf16),
                    spec(per, NST + 2 * EDGE, width, dtype=bf16),
                    spec(per, EDGE, wide),
                ],
                [pltpu.VMEM((rows + EDGE, wide), f32), pltpu.VMEM((NST, width), f32)],
                2 * per * rows * model * w_all.shape[1],
            )
        )
    entering = [exchange(first[g][7], "seq", True) for g in range(GROUPS)]

    second = []
    for g in range(GROUPS):
        part = slice(g * per, (g + 1) * per)
        _, proj, _, acted, own, cumul, _, _, _ = first[g]
        second.append(
            run(
                gate_kernel,
                "gate",
                per,
                [acted, own, cumul, proj[:, :, :width], entering[g], grad_branch[part]],
                [w_back, spread, chan],
                [
                    spec(per, rows, width, dtype=bf16),
                    spec(per, rows, width, dtype=bf16),
                    spec(per, EDGE, rows),
                ],
                [],
                2 * per * rows * model * width,
            )
        )
    sums = [lax.psum(second[g][2], "head") for g in range(GROUPS)]

    third = []
    for g in range(GROUPS):
        _, proj, dt_raw, acted, _, cumul, states, _, _ = first[g]
        ssd, gn, _ = second[g]
        third.append(
            run(
                functools.partial(mixer_kernel, inner_total=inner_total),
                "mixer",
                per,
                [
                    sums[g],
                    ssd,
                    proj[:, :, :width],
                    gn,
                    acted,
                    dt_raw,
                    cumul,
                    states,
                    entering[g],
                ],
                [w_back, head_rows, spread, chan],
                [
                    spec(per, rows, width, dtype=bf16),
                    spec(per, rows, model, dtype=bf16),
                    spec(per, rows, width, dtype=bf16),
                    spec(per, rows, width, dtype=bf16),
                    spec(per, rows, 2 * NST),
                    spec(per, rows, LANES),
                    spec(per, rows, LANES),
                    spec(per, NST, width, dtype=bf16),
                    spec(per, EDGE, width),
                ],
                [pltpu.VMEM((NST, width), f32)],
                2 * per * rows * model * width,
            )
        )
    branches = [lax.psum(third[g][1], "head") for g in range(GROUPS)]
    leaving = [
        exchange(
            jnp.concatenate([third[g][7], first[g][7][:, NST:]], axis=1), "seq", False
        )
        for g in range(GROUPS)
    ]

    fourth = []
    for g in range(GROUPS):
        _, proj, dt_raw, acted, _, cumul, _, _, edge = first[g]
        _, _, _, dx, dbc, ddt, dld, _, _ = third[g]
        fourth.append(
            run(
                conv_kernel,
                "conv",
                per,
                [proj, edge, acted, dx, dbc, ddt, dld, dt_raw, cumul, entering[g], leaving[g]],
                [taps, head_rows, spread],
                [
                    spec(per, rows, wide, dtype=bf16),
                    spec(per, rows, LANES, dtype=bf16),
                    spec(per, EDGE, wide),
                    spec(per, EDGE, wide),
                    spec(per, EDGE, LANES),
                ],
                [pltpu.VMEM((rows + EDGE, wide), f32), pltpu.VMEM((rows + EDGE, wide), f32)],
                per * rows * wide * 60,
            )
        )
    nexts = [
        lax.ppermute(fourth[g][2], "seq", [(i + 1, i) for i in range(seq_size - 1)])
        for g in range(GROUPS)
    ]

    fifth = []
    for g in range(GROUPS):
        gj, gdt, _, _, _ = fourth[g]
        fifth.append(
            run(
                input_kernel,
                "input_grad",
                per,
                [third[g][2], gj, gdt, nexts[g]],
                [taps, w_all],
                [spec(per, rows, wide, dtype=bf16), spec(per, rows, model, dtype=bf16)],
                [],
                2 * per * rows * model * w_all.shape[1],
            )
        )
    summed = [lax.psum(fifth[g][1], "head") for g in range(GROUPS)]

    def joined(parts):
        return jnp.concatenate(parts, axis=0).reshape(batch * rows, -1)

    normed = joined([f[0] for f in first])
    gz = joined([t[2] for t in third])
    gj = joined([t[0] for t in fifth])
    gdt = joined([t[1] for t in fourth])
    gnorm = joined([t[0] for t in third])
    w_grad = jnp.concatenate(
        [mm(normed, gz, TN), mm(normed, gj, TN), mm(normed, gdt, TN)], axis=1
    ).astype(bf16)
    out_w_grad = mm(gnorm, grad_branch.reshape(batch * rows, model), TN).astype(bf16)
    w_sum = lax.psum_scatter(w_grad, "seq", scatter_dimension=0, tiled=True)
    out_w_sum = lax.psum_scatter(out_w_grad, "seq", scatter_dimension=1, tiled=True)
    bc_sum = lax.psum(w_sum[:, 2 * width : 2 * width + 2 * NST], "head")

    layer_outs = []
    input_grads = []
    gain_grad = jnp.zeros((model,), f32)
    for g in range(GROUPS):
        part = slice(g * per, (g + 1) * per)
        hidden = flat[part].astype(f32)
        layer_outs.append(
            jnp.where(
                valid[part][:, :, None], hidden + branches[g].astype(f32), hidden
            ).astype(bf16)
        )
        inverse = lax.rsqrt(jnp.mean(hidden * hidden, axis=-1, keepdims=True) + epsilon)
        unit = hidden * inverse
        grad_in = summed[g].astype(f32)
        gain_grad = gain_grad + jnp.sum(grad_in * unit, axis=(0, 1))
        scaled = grad_in * norm_gain
        input_grads.append(
            (
                flat_grad[part].astype(f32)
                + inverse * (scaled - unit * jnp.mean(scaled * unit, axis=-1, keepdims=True))
            ).astype(bf16)
        )

    cols = sum(jnp.sum(t[8], axis=0) for t in third)
    tap_sum = sum(jnp.sum(t[3], axis=0) for t in fourth)
    head_sum = sum(jnp.sum(t[4], axis=0) for t in fourth)
    skip = jnp.sum(cols[1].reshape(heads, HEAD_DIM), axis=1)
    gain_grad, cols0, tap_sum, head_sum, skip = lax.psum(
        (gain_grad, cols[0], tap_sum[: CONV + 1], head_sum[:2], skip), "seq"
    )
    bc_taps = lax.psum(tap_sum[:, width:], "head")

    out_shape = (micro, seqs, rows, model)
    return (
        jnp.concatenate(layer_outs, axis=0).reshape(out_shape),
        jnp.concatenate(input_grads, axis=0).reshape(out_shape),
        gain_grad,
        w_sum[:, :width].astype(f32),
        w_sum[:, width : 2 * width].astype(f32),
        bc_sum.astype(f32),
        w_sum[:, 2 * width + 2 * NST : 2 * width + 2 * NST + heads].astype(f32),
        tap_sum[:CONV, :width],
        tap_sum[CONV, :width],
        bc_taps[:CONV],
        bc_taps[CONV],
        head_sum[0, :heads],
        head_sum[1, :heads],
        skip,
        cols0,
        out_w_sum.astype(f32),
    )


def solution(mesh):
    placed = (
        P(None, None, "seq", None),
        P(),
        P("seq", "head"),
        P("seq", "head"),
        P("seq", None),
        P("seq", "head"),
        P(None, "head"),
        P("head"),
        P(),
        P(),
        P("head"),
        P("head"),
        P("head"),
        P("head"),
        P("head", "seq"),
        P(),
        P(None, None, "seq", None),
    )
    return jax.shard_map(
        local,
        mesh=mesh,
        in_specs=placed,
        out_specs=(
            P(None, None, "seq", None),
            P(None, None, "seq", None),
            P(),
            P("seq", "head"),
            P("seq", "head"),
            P("seq", None),
            P("seq", "head"),
            P(None, "head"),
            P("head"),
            P(),
            P(),
            P("head"),
            P("head"),
            P("head"),
            P("head"),
            P("head", "seq"),
        ),
        check_vma=False,
    )
```

time: 1810 us -> 1120 us (0.62)
  matrix products: 420 us -> 35 us
  Pallas kernels: 0 us -> 236 us
  other arithmetic: 287 us -> 63.9 us
  local copies, waits for them, and re-layouts: 259 us -> 56 us
  waiting for transfers between devices: 709 us -> 645 us
  blocking collectives: 94.1 us -> 34.9 us
  starting transfers between devices: 9.79 us -> 28.6 us
    dot_general x96 -> x4, matrix products: 420 us -> 35 us  [mm(): return lax.dot_general(a, b, dims, preferred_element_type=f32)]
    pallas_call x0 -> x20, Pallas kernels: none -> 236 us  [run(): pl.pallas_call(body, name=name, grid=(count,), in_specs=[per_sequence(a.s...]
    reduce_scatter x8 -> x1, waiting for transfers between devices: 189 us -> 40.8 us  [local(): lax.psum_scatter(out_w_grad, 'seq', scatter_dimension=1, tiled=True)]
    another operation x70 -> x0, other arithmetic: 80.1 us -> none
    another operation x144 -> x3, local copies, waits for them, and re-layouts: 55.9 us -> 0.15 us  [the longest x1 0.08 us: local(): jnp.repeat(d_skip, HEAD_DIM)[None]]
    reduce_sum x19 -> x22, other arithmetic: 62.6 us -> 8.54 us  [the longest x1 6.72 us: local(): gain_grad = gain_grad + jnp.sum(grad_in * unit, axis=(0, 1))]
    all_gather x7 -> x2, waiting for transfers between devices: 8.45 us -> 49.5 us  [the longest x1 41.4 us: local(): w_all = lax.all_gather(w_shard, 'seq', axis=0, tiled=True)]
    all_gather x4 -> x0, blocking collectives: 38.4 us -> none  [the longest x2 17 us: prefix(): lax.all_gather(part.astype(kind), axis)]
  transfers between devices with their start and end apart: 22 -> 35, of which waited for: 9 -> 13; matrix products, arithmetic and copies ran while one was open for 28% -> 8% of each run, Pallas kernels for 0% -> 16%
where the time goes in v1:
time: 1120 us; the launch traced here: 1110 us
  waiting for transfers between devices  645 us (58%)
  Pallas kernels  236 us (21%)
  other arithmetic  63.9 us (6%)
  local copies, waits for them, and re-layouts  56 us (5%)
  matrix products  35 us (3%)
  blocking collectives  34.9 us (3%)
  starting transfers between devices  28.6 us (3%)
  between operations  16.1 us (1%)
    psum x1, waiting for transfers between devices, local(): bc_sum = lax.psum(w_sum[:, 2 * width:2 * width + 2 * NST], 'head')  435 us
    pallas_call x20, Pallas kernels, run(): pl.pallas_call(body, name=name, grid=(count,), in_specs=[per_sequence(a.s...  236 us
    unnamed x7, waiting for transfers between devices  50.3 us
    all_gather x1, waiting for transfers between devices, local(): w_all = lax.all_gather(w_shard, 'seq', axis=0, tiled=True)  41.4 us
    reduce_scatter x1, waiting for transfers between devices, local(): lax.psum_scatter(out_w_grad, 'seq', scatter_dimension=1, tiled=True)  40.8 us
    ppermute x24, waiting for transfers between devices, exchange(): got = lax.ppermute(payload, axis, [(i, i ^ bit) for i in range(size)])  36 us
    dot_general x4, matrix products, mm(): return lax.dot_general(a, b, dims, preferred_element_type=f32)  35 us
    psum x1, waiting for transfers between devices, local(): sums = [lax.psum(second[g][2], 'head') for g in range(GROUPS)]  33 us
  transfers between devices with their start and end apart: 35, of which 13 were waited for; matrix products, arithmetic and copies ran while one was open for 8% of the time, Pallas kernels for 16%

profile of v1, /device:TPU:0, one launch (start us, length us, event | category | flops | bytes accessed | tf_op | source)
XLA Modules:
  0.0 1114.9 jit_solution(12675070412404233106)
XLA Ops:
  46.1 41.4 %all-gather.3.cloned.1.call-done.w_ref = bf16[1536,1920]{1,0:T(8,128)(2,1)} async-done(((bf16[192,1920]{1,0:T(8,128)(2,1)}), bf16[1536,1920]{1,0:T(8,128)(2,1)}) %all-gather.3.cloned.1.call-update) | async-done | bytes 5898256 | tf_op jit(solution)/shard_map/all_gather | solution.py:584
  87.5 15.0 %project.4 = (bf16[1,512,1536]{2,1,0:T(8,128)(2,1)}, bf16[1,512,1792]{2,1,0:T(8,128)(2,1)}, f32[1,512,128]{2,1,0:T(8,128)}, bf16[1,512,1024]{2,1,0:T(8,128)(2,1)...) custom-call(bf16[1,512,1536]{2,1,0:T(8,128)(2,1)} %get-tuple-element, ...), custom_call_target="tpu_custom_call" | custom-call | flops 3019898880 | bytes 14567424 | tf_op jit(solution)/shard_map/project/pallas_call | solution.py:499
  103.6 15.0 %project.7 = (bf16[1,512,1536]{2,1,0:T(8,128)(2,1)}, bf16[1,512,1792]{2,1,0:T(8,128)(2,1)}, f32[1,512,128]{2,1,0:T(8,128)}, bf16[1,512,1024]{2,1,0:T(8,128)(2,1)...) custom-call(bf16[1,512,1536]{2,1,0:T(8,128)(2,1)} %get-tuple-element, ...), custom_call_target="tpu_custom_call" | custom-call | flops 3019898880 | bytes 14567424 | tf_op jit(solution)/shard_map/project/pallas_call | solution.py:499
  119.6 14.9 %project.6 = (bf16[1,512,1536]{2,1,0:T(8,128)(2,1)}, bf16[1,512,1792]{2,1,0:T(8,128)(2,1)}, f32[1,512,128]{2,1,0:T(8,128)}, bf16[1,512,1024]{2,1,0:T(8,128)(2,1)...) custom-call(bf16[1,512,1536]{2,1,0:T(8,128)(2,1)} %get-tuple-element, ...), custom_call_target="tpu_custom_call" | custom-call | flops 3019898880 | bytes 14567424 | tf_op jit(solution)/shard_map/project/pallas_call | solution.py:499
  134.8 14.9 %project.5 = (bf16[1,512,1536]{2,1,0:T(8,128)(2,1)}, bf16[1,512,1792]{2,1,0:T(8,128)(2,1)}, f32[1,512,128]{2,1,0:T(8,128)}, bf16[1,512,1024]{2,1,0:T(8,128)(2,1)...) custom-call(bf16[1,512,1536]{2,1,0:T(8,128)(2,1)} %get-tuple-element, ...), custom_call_target="tpu_custom_call" | custom-call | flops 3019898880 | bytes 14567424 | tf_op jit(solution)/shard_map/project/pallas_call | solution.py:499
  226.0 33.0 %all-reduce.8.cloned.1.call-done = (f32[1,8,512]{2,1,0:T(8,128)}, f32[1,8,512]{2,1,0:T(8,128)}, f32[1,8,512]{2,1,0:T(8,128)}, f32[1,8,512]{2,1,0:T(8,128)}) async-done(((f32[1,8,512]{2,1,0:T(8,128)}, f32[1,8,512]{2,1,0:T(8,128)}, f32[1,8,512]{2,1,0:T(8,128)}, f32[1,8,512]{2,1,0:T(8,128)}), (f32[1,8,512]{2,1,0:T(8,128)}, f32[1,8,512]{2,1,0:T(8,128)}, f32[1,8,512]{2,1,0:T(8,128)}, ...) | async-done | bytes 65552 | tf_op jit(solution)/shard_map/psum | solution.py:668
  259.1 16.0 %mixer.4 = (bf16[1,512,768]{2,1,0:T(8,128)(2,1)}, bf16[1,512,1536]{2,1,0:T(8,128)(2,1)}, bf16[1,512,768]{2,1,0:T(8,128)(2,1)}, bf16[1,512,768]{2,1,0:T(8,128)(2,...) custom-call(f32[1,8,512]{2,1,0:T(8,128)} %get-tuple-element.304.sums, ...), custom_call_target="tpu_custom_call" | custom-call | flops 1207959552 | bytes 12718080 | tf_op jit(solution)/shard_map/mixer/pallas_call | solution.py:499
  276.1 15.8 %mixer.7 = (bf16[1,512,768]{2,1,0:T(8,128)(2,1)}, bf16[1,512,1536]{2,1,0:T(8,128)(2,1)}, bf16[1,512,768]{2,1,0:T(8,128)(2,1)}, bf16[1,512,768]{2,1,0:T(8,128)(2,...) custom-call(f32[1,8,512]{2,1,0:T(8,128)} %get-tuple-element.301.sums, ...), custom_call_target="tpu_custom_call" | custom-call | flops 1207959552 | bytes 12718080 | tf_op jit(solution)/shard_map/mixer/pallas_call | solution.py:499
  293.9 15.7 %mixer.6 = (bf16[1,512,768]{2,1,0:T(8,128)(2,1)}, bf16[1,512,1536]{2,1,0:T(8,128)(2,1)}, bf16[1,512,768]{2,1,0:T(8,128)(2,1)}, bf16[1,512,768]{2,1,0:T(8,128)(2,...) custom-call(f32[1,8,512]{2,1,0:T(8,128)} %get-tuple-element.302.sums, ...), custom_call_target="tpu_custom_call" | custom-call | flops 1207959552 | bytes 12718080 | tf_op jit(solution)/shard_map/mixer/pallas_call | solution.py:499
  311.3 16.3 %mixer.5 = (bf16[1,512,768]{2,1,0:T(8,128)(2,1)}, bf16[1,512,1536]{2,1,0:T(8,128)(2,1)}, bf16[1,512,768]{2,1,0:T(8,128)(2,1)}, bf16[1,512,768]{2,1,0:T(8,128)(2,...) custom-call(f32[1,8,512]{2,1,0:T(8,128)} %get-tuple-element.303.sums, ...), custom_call_target="tpu_custom_call" | custom-call | flops 1207959552 | bytes 12718080 | tf_op jit(solution)/shard_map/mixer/pallas_call | solution.py:499
  367.5 11.5 %conv.4 = (bf16[1,512,1024]{2,1,0:T(8,128)(2,1)}, bf16[1,512,128]{2,1,0:T(8,128)(2,1)}, f32[1,8,1024]{2,1,0:T(8,128)}, f32[1,8,1024]{2,1,0:T(8,128)}, f32[1,8,128]{2,1,0:T(8,128)}) custom-call(bf16[1,512,1792]{2,1,0:T(8,128)(2,1)} %get-tuple-element.131.proj_ref, f32[1,8,1024]{2,1,0:T(8,128)} %get-tuple-element.173.edge_ref, ...), custom_call_target="tpu_custom_call" | custom-call | flops 31457280 | bytes 7151616 | tf_op jit(solution)/shard_map/conv/pallas_call | solution.py:499
  387.6 8.9 input_grad.4
  398.2 11.4 %conv.5 = (bf16[1,512,1024]{2,1,0:T(8,128)(2,1)}, bf16[1,512,128]{2,1,0:T(8,128)(2,1)}, f32[1,8,1024]{2,1,0:T(8,128)}, f32[1,8,1024]{2,1,0:T(8,128)}, f32[1,8,128]{2,1,0:T(8,128)}) custom-call(bf16[1,512,1792]{2,1,0:T(8,128)(2,1)} %get-tuple-element.142.proj_ref, f32[1,8,1024]{2,1,0:T(8,128)} %get-tuple-element.184.edge_ref, ...), custom_call_target="tpu_custom_call" | custom-call | flops 31457280 | bytes 7151616 | tf_op jit(solution)/shard_map/conv/pallas_call | solution.py:499
  412.7 11.5 %conv.6 = (bf16[1,512,1024]{2,1,0:T(8,128)(2,1)}, bf16[1,512,128]{2,1,0:T(8,128)(2,1)}, f32[1,8,1024]{2,1,0:T(8,128)}, f32[1,8,1024]{2,1,0:T(8,128)}, f32[1,8,128]{2,1,0:T(8,128)}) custom-call(bf16[1,512,1792]{2,1,0:T(8,128)(2,1)} %get-tuple-element.153.proj_ref, f32[1,8,1024]{2,1,0:T(8,128)} %get-tuple-element.195.edge_ref, ...), custom_call_target="tpu_custom_call" | custom-call | flops 31457280 | bytes 7151616 | tf_op jit(solution)/shard_map/conv/pallas_call | solution.py:499
  426.3 11.5 %conv.7 = (bf16[1,512,1024]{2,1,0:T(8,128)(2,1)}, bf16[1,512,128]{2,1,0:T(8,128)(2,1)}, f32[1,8,1024]{2,1,0:T(8,128)}, f32[1,8,1024]{2,1,0:T(8,128)}, f32[1,8,128]{2,1,0:T(8,128)}) custom-call(bf16[1,512,1792]{2,1,0:T(8,128)(2,1)} %get-tuple-element.164.proj_ref, f32[1,8,1024]{2,1,0:T(8,128)} %get-tuple-element.206.edge_ref, ...), custom_call_target="tpu_custom_call" | custom-call | flops 31457280 | bytes 7151616 | tf_op jit(solution)/shard_map/conv/pallas_call | solution.py:499
  443.8 8.9 input_grad.5
  453.3 9.0 input_grad.6
  471.7 10.9 bitcast_convert_fusion
  495.8 11.4 %bitcast_convert_fusion.1 = bf16[768,1536]{0,1:T(8,128)(2,1)} fusion(bf16[4,512,1536]{2,1,0:T(8,128)(2,1)} %copy-done, bf16[1,512,768]{2,1,0:T(8,128)(2,1)S(1)} %copy-done.46, bf16[1,512,768]{2,1,0:T(8,128)(2,1)S(1)} %copy-done.47, bf16[1,512,768]{2,1,0:T(8,128)(2,1)S(1)} %copy-done.48, bf16[1,512,768]{2,1,0:T(8,128)(2,1)S(1)} %copy-done.45), kind=kOutput, calls=%fused_computation.21 | convolution fusion | flops 4837736448 | bytes 11796480 | tf_op jit(solution)/shard_map/dot_general | solution.py:28
  507.3 49.5 %reduce-scatter.7.cloned.1.call-done = bf16[192,1920]{1,0:T(8,128)(2,1)} async-done(((bf16[1536,1920]{1,0:T(8,128)(2,1)}), bf16[192,1920]{1,0:T(8,128)(2,1)}) %reduce-scatter.7.cloned.1.call-update) | async-done | bytes 737296
  562.7 40.8 %reduce-scatter.5.cloned.1.call-done = bf16[768,192]{0,1:T(8,128)(2,1)} async-done(((bf16[768,1536]{0,1:T(8,128)(2,1)}), bf16[768,192]{0,1:T(8,128)(2,1)}) %reduce-scatter.5.cloned.1.call-update) | async-done | bytes 294928 | tf_op jit(solution)/shard_map/reduce_scatter | solution.py:771
  608.3 435.2 %all-reduce.10.cloned.1.call-done = (bf16[192,256]{0,1:T(8,128)(2,1)}, bf16[1,512,1536]{2,1,0:T(8,128)(2,1)}, bf16[1,512,1536]{2,1,0:T(8,128)(2,1)}, bf16[1,512,...) async-done(((bf16[192,256]{0,1:T(8,128)(2,1)}, ...) | async-done | bytes 12681232 | tf_op jit(solution)/shard_map/psum | solution.py:772
  1050.3 25.1 %all-reduce.2 = (f32[1536]{0:T(1024)}, f32[5,1024]{1,0:T(8,128)S(1)}, f32[2,128]{1,0:T(2,128)S(1)}, f32[12]{0:T(128)}, f32[768]{0:T(1024)}) all-reduce(f32[1536]{0:T(1024)S(1)} %add_add_fusion.1, f32[5,1024]{1,0:T(8,128)S(1)} %fusion.122, f32[2,128]{1,0:T(2,128)S(1)} %slice_bitcast_fusion, ...), channel_id=1, replica_groups=mesh['seq'=8,'head'=4] {'seq'}, use_global_device_ids=true, to_apply=%region_44.45 | all-reduce | flops 7692 | bytes 61536 | tf_op jit(solution)/shard_map/psum | solution.py:801
  1075.4 9.8 psum.148
  (387 shorter events, 245.5 us)
Async XLA Ops:
  7.2 34.5 %all-gather.5.cloned.1.call-start = ((), (), s32[]{:S(2)}) async-start(), calls=%async_computation.3 | async-start | bytes 2654208 | tf_op jit(solution)/shard_map/all_gather | solution.py:585
  8.0 79.6 %all-gather.3.cloned.1.call-start = ((), (), s32[]{:S(2)}) async-start(), calls=%async_computation.2 | async-start | bytes 6635520 | tf_op jit(solution)/shard_map/all_gather | solution.py:584
  10.9 248.2 %all-reduce.8.cloned.1.call-start = ((), (), s32[]{:S(2)}) async-start(), calls=%async_computation.6 | async-start | bytes 131072 | tf_op jit(solution)/shard_map/psum | solution.py:668
  11.9 21.0 %collective-permute-start = (bf16[4,16,1536]{2,1,0:T(8,128)(2,1)S(1)}, bf16[4,16,1536]{2,1,0:T(8,128)(2,1)S(1)}, u32[]{:S(2)}, u32[]{:S(2)}) collective-permute-start(bf16[4,16,1536]{2,1,0:T(8,128)(2,1)S(1)} %slice.396), channel_id=1, source_target_pairs={{0,4},{4,8},{8,12},{12,16},{16,20},{20,24},{24,28},{1,5},{5,9},{9,... | collective-permute-start | bytes 589832 | tf_op jit(solution)/shard_map/ppermute | solution.py:575
  102.6 57.6 %collective-permute-start.1 = (bf16[1,144,768]{2,1,0:T(8,128)(2,1)}, bf16[1,144,768]{2,1,0:T(8,128)(2,1)S(1)}, u32[]{:S(2)}, u32[]{:S(2)}) collective-permute-start(bf16[1,144,768]{2,1,0:T(8,128)(2,1)} %get-tuple-element.132), channel_id=1, source_target_pairs={{0,4},{4,0},{8,12},{12,8},{16,20},{20,16},{24,28},{28,24},{1,5},{5... | collective-permute-start | bytes 663560 | tf_op jit(solution)/shard_map/ppermute | solution.py:526
  118.6 41.8 %collective-permute-start.10 = (bf16[1,144,768]{2,1,0:T(8,128)(2,1)}, bf16[1,144,768]{2,1,0:T(8,128)(2,1)S(1)}, u32[]{:S(2)}, u32[]{:S(2)}) collective-permute-start(bf16[1,144,768]{2,1,0:T(8,128)(2,1)} %get-tuple-element.165), channel_id=1, source_target_pairs={{0,4},{4,0},{8,12},{12,8},{16,20},{20,16},{24,28},{28,24},{1,5},{5... | collective-permute-start | bytes 663560 | tf_op jit(solution)/shard_map/ppermute | solution.py:526
  134.5 25.7 %collective-permute-start.7 = (bf16[1,144,768]{2,1,0:T(8,128)(2,1)}, bf16[1,144,768]{2,1,0:T(8,128)(2,1)S(1)}, u32[]{:S(2)}, u32[]{:S(2)}) collective-permute-start(bf16[1,144,768]{2,1,0:T(8,128)(2,1)} %get-tuple-element.154), channel_id=1, source_target_pairs={{0,4},{4,0},{8,12},{12,8},{16,20},{20,16},{24,28},{28,24},{1,5},{5... | collective-permute-start | bytes 663560 | tf_op jit(solution)/shard_map/ppermute | solution.py:526
  168.8 21.0 %collective-permute-start.3 = (bf16[1,144,768]{2,1,0:T(8,128)(2,1)S(1)}, bf16[1,144,768]{2,1,0:T(8,128)(2,1)S(1)}, u32[]{:S(2)}, u32[]{:S(2)}) collective-permute-start(bf16[1,144,768]{2,1,0:T(8,128)(2,1)S(1)} %get-tuple-element.377), channel_id=1, source_target_pairs={{0,16},{4,20},{8,24},{12,28},{16,0},{20,4},{24,8},{28,12},{1,17},{... | collective-permute-start | bytes 663560 | tf_op jit(solution)/shard_map/ppermute | solution.py:526
  172.1 13.9 %collective-permute-start.8 = (bf16[1,144,768]{2,1,0:T(8,128)(2,1)S(1)}, bf16[1,144,768]{2,1,0:T(8,128)(2,1)S(1)}, u32[]{:S(2)}, u32[]{:S(2)}) collective-permute-start(bf16[1,144,768]{2,1,0:T(8,128)(2,1)S(1)} %get-tuple-element.379), channel_id=1, source_target_pairs={{0,8},{4,12},{8,0},{12,4},{16,24},{20,28},{24,16},{28,20},{1,9},{5... | collective-permute-start | bytes 663560 | tf_op jit(solution)/shard_map/ppermute | solution.py:526
  189.0 27.1 %collective-permute-start.12 = (bf16[1,144,768]{2,1,0:T(8,128)(2,1)S(1)}, bf16[1,144,768]{2,1,0:T(8,128)(2,1)S(1)}, u32[]{:S(2)}, u32[]{:S(2)}) collective-permute-start(bf16[1,144,768]{2,1,0:T(8,128)(2,1)S(1)} %get-tuple-element.383), channel_id=1, source_target_pairs={{0,16},{4,20},{8,24},{12,28},{16,0},{20,4},{24,8},{28,12},{1,17},{... | collective-permute-start | bytes 663560 | tf_op jit(solution)/shard_map/ppermute | solution.py:526
  224.7 332.1 %reduce-scatter.7.cloned.1.call-start = ((), (), s32[]{:S(2)}) async-start(), calls=%async_computation.5 | async-start | bytes 6635520
  276.0 61.9 %collective-permute-start.13 = (bf16[1,144,768]{2,1,0:T(8,128)(2,1)S(1)}, bf16[1,144,768]{2,1,0:T(8,128)(2,1)S(1)}, u32[]{:S(2)}, u32[]{:S(2)}) collective-permute-start(bf16[1,144,768]{2,1,0:T(8,128)(2,1)S(1)} %pad_maximum_fusion.3), channel_id=1, source_target_pairs={{0,4},{4,0},{8,12},{12,8},{16,20},{20,16},{24,28},{28,24},{1,5},{5... | collective-permute-start | bytes 663560 | tf_op jit(solution)/shard_map/ppermute | solution.py:526
  293.4 44.5 %collective-permute-start.25 = (bf16[1,144,768]{2,1,0:T(8,128)(2,1)}, bf16[1,144,768]{2,1,0:T(8,128)(2,1)S(1)}, u32[]{:S(2)}, u32[]{:S(2)}) collective-permute-start(bf16[1,144,768]{2,1,0:T(8,128)(2,1)} %pad_maximum_fusion.6), channel_id=1, source_target_pairs={{0,4},{4,0},{8,12},{12,8},{16,20},{20,16},{24,28},{28,24},{1,5},{5... | collective-permute-start | bytes 663560 | tf_op jit(solution)/shard_map/ppermute | solution.py:526
  311.2 26.8 %collective-permute-start.21 = (bf16[1,144,768]{2,1,0:T(8,128)(2,1)}, bf16[1,144,768]{2,1,0:T(8,128)(2,1)S(1)}, u32[]{:S(2)}, u32[]{:S(2)}) collective-permute-start(bf16[1,144,768]{2,1,0:T(8,128)(2,1)} %pad_maximum_fusion.5), channel_id=1, source_target_pairs={{0,4},{4,0},{8,12},{12,8},{16,20},{20,16},{24,28},{28,24},{1,5},{5... | collective-permute-start | bytes 663560 | tf_op jit(solution)/shard_map/ppermute | solution.py:526
  346.3 20.3 %collective-permute-start.15 = (bf16[1,144,768]{2,1,0:T(8,128)(2,1)S(1)}, bf16[1,144,768]{2,1,0:T(8,128)(2,1)S(1)}, u32[]{:S(2)}, u32[]{:S(2)}) collective-permute-start(bf16[1,144,768]{2,1,0:T(8,128)(2,1)S(1)} %get-tuple-element.370), channel_id=1, source_target_pairs={{0,16},{4,20},{8,24},{12,28},{16,0},{20,4},{24,8},{28,12},{1,17},{... | collective-permute-start | bytes 663560 | tf_op jit(solution)/shard_map/ppermute | solution.py:526
  349.4 14.9 %collective-permute-start.26 = (bf16[1,144,768]{2,1,0:T(8,128)(2,1)S(1)}, bf16[1,144,768]{2,1,0:T(8,128)(2,1)S(1)}, u32[]{:S(2)}, u32[]{:S(2)}) collective-permute-start(bf16[1,144,768]{2,1,0:T(8,128)(2,1)S(1)} %get-tuple-element.373), channel_id=1, source_target_pairs={{0,8},{4,12},{8,0},{12,4},{16,24},{20,28},{24,16},{28,20},{1,9},{5... | collective-permute-start | bytes 663560 | tf_op jit(solution)/shard_map/ppermute | solution.py:526
  349.9 13.7 %collective-permute-start.22 = (bf16[1,144,768]{2,1,0:T(8,128)(2,1)S(1)}, bf16[1,144,768]{2,1,0:T(8,128)(2,1)S(1)}, u32[]{:S(2)}, u32[]{:S(2)}) collective-permute-start(bf16[1,144,768]{2,1,0:T(8,128)(2,1)S(1)} %get-tuple-element.372), channel_id=1, source_target_pairs={{0,8},{4,12},{8,0},{12,4},{16,24},{20,28},{24,16},{28,20},{1,9},{5... | collective-permute-start | bytes 663560 | tf_op jit(solution)/shard_map/ppermute | solution.py:526
  384.9 26.0 %collective-permute-start.23 = (bf16[1,144,768]{2,1,0:T(8,128)(2,1)}, bf16[1,144,768]{2,1,0:T(8,128)(2,1)}, u32[]{:S(2)}, u32[]{:S(2)}) collective-permute-start(bf16[1,144,768]{2,1,0:T(8,128)(2,1)} %get-tuple-element.375), channel_id=1, source_target_pairs={{0,16},{4,20},{8,24},{12,28},{16,0},{20,4},{24,8},{28,12},{1,17},{... | collective-permute-start | bytes 663560 | tf_op jit(solution)/shard_map/ppermute | solution.py:526
  385.8 39.7 %collective-permute-start.27 = (bf16[1,144,768]{2,1,0:T(8,128)(2,1)}, bf16[1,144,768]{2,1,0:T(8,128)(2,1)S(1)}, u32[]{:S(2)}, u32[]{:S(2)}) collective-permute-start(bf16[1,144,768]{2,1,0:T(8,128)(2,1)} %get-tuple-element.376), channel_id=1, source_target_pairs={{0,16},{4,20},{8,24},{12,28},{16,0},{20,4},{24,8},{28,12},{1,17},{... | collective-permute-start | bytes 663560 | tf_op jit(solution)/shard_map/ppermute | solution.py:526
  409.6 33.5 %collective-permute-start.20 = (f32[1,8,1024]{2,1,0:T(8,128)}, f32[1,8,1024]{2,1,0:T(8,128)S(1)}, u32[]{:S(2)}, u32[]{:S(2)}) collective-permute-start(f32[1,8,1024]{2,1,0:T(8,128)} %get-tuple-element.192), channel_id=1, source_target_pairs={{4,0},{8,4},{12,8},{16,12},{20,16},{24,20},{28,24},{5,1},{9,5},{13... | collective-permute-start | bytes 98312 | tf_op jit(solution)/shard_map/ppermute | solution.py:737
  424.2 28.5 %collective-permute-start.24 = (f32[1,8,1024]{2,1,0:T(8,128)}, f32[1,8,1024]{2,1,0:T(8,128)S(1)}, u32[]{:S(2)}, u32[]{:S(2)}) collective-permute-start(f32[1,8,1024]{2,1,0:T(8,128)} %get-tuple-element.203), channel_id=1, source_target_pairs={{4,0},{8,4},{12,8},{16,12},{20,16},{24,20},{28,24},{5,1},{9,5},{13... | collective-permute-start | bytes 98312 | tf_op jit(solution)/shard_map/ppermute | solution.py:737
  437.8 24.5 %collective-permute-start.28 = (f32[1,8,1024]{2,1,0:T(8,128)}, f32[1,8,1024]{2,1,0:T(8,128)S(1)}, u32[]{:S(2)}, u32[]{:S(2)}) collective-permute-start(f32[1,8,1024]{2,1,0:T(8,128)} %get-tuple-element.214), channel_id=1, source_target_pairs={{4,0},{8,4},{12,8},{16,12},{20,16},{24,20},{28,24},{5,1},{9,5},{13... | collective-permute-start | bytes 98312 | tf_op jit(solution)/shard_map/ppermute | solution.py:737
  494.0 109.4 %reduce-scatter.5.cloned.1.call-start = ((), (), s32[]{:S(2)}) async-start(), calls=%async_computation.4 | async-start | bytes 2654208 | tf_op jit(solution)/shard_map/reduce_scatter | solution.py:771
  507.3 536.3 %all-reduce.10.cloned.1.call-start = ((), (), s32[]{:S(2)}) async-start(), calls=%async_computation.7 | async-start | bytes 25427968 | tf_op jit(solution)/shard_map/psum | solution.py:772
  (72 other events, 1174.3 us)
Sparse Core Ops, SparseCore 0:
  10.0 31.7 all-gather.4
  43.6 43.8 all-gather.2
  224.8 34.1 all-reduce.7
  494.2 62.6 reduce-scatter.6
  561.0 42.4 reduce-scatter.4
  607.6 435.8 all-reduce.9

commit v2 on v1

--- a/solution.py
+++ b/solution.py
@@ -14,6 +14,7 @@
 LANES = 128
 EDGE = 8
 GROUPS = 4
+PIECES = 8
 
 epsilon = 1e-05
 f32 = jnp.float32
@@ -197,7 +198,7 @@
 ):
     rows = acted_ref.shape[1]
     width = spread_ref.shape[1]
-    gn_ref[0] = mm(grad_ref[0], w_out_ref[...], NT).astype(bf16)
+    gn_ref[0] = mm(grad_ref[0], w_out_ref[...]).astype(bf16)
 
     def chunk(index, carry):
         here = pl.ds(pl.multiple_of(index * CHUNK, CHUNK), CHUNK)
@@ -368,7 +369,7 @@
 
     lax.fori_loop(0, chunks, chunk, 0)
     total_ref[0] = grad_state[...].astype(bf16)
-    branch_ref[0] = mm(gnorm_ref[0], w_out_ref[...]).astype(bf16)
+    branch_ref[0] = mm(gnorm_ref[0], w_out_ref[...], NT).astype(bf16)
 
 
 def conv_kernel(
@@ -542,6 +543,467 @@
     return met.astype(bf16)
 
 
+MESH = pl.DeviceIdType.MESH
+
+
+def gather_kernel(shard_ref, full_ref, own_sem, send, recv, pass_send, pass_recv):
+    size = lax.axis_size("seq")
+    me = lax.axis_index("seq")
+    rows = shard_ref.shape[0]
+    partner = me ^ 1
+
+    def at(ref, owner):
+        return ref.at[pl.ds(pl.multiple_of(owner * rows, 16), rows), :]
+
+    def direct(k, owner, peer):
+        return pltpu.make_async_remote_copy(
+            src_ref=shard_ref,
+            dst_ref=at(full_ref, owner),
+            send_sem=send.at[k],
+            recv_sem=recv.at[k],
+            device_id={"seq": peer},
+            device_id_type=MESH,
+        )
+
+    def passed(k, owner):
+        return pltpu.make_async_remote_copy(
+            src_ref=at(full_ref, owner),
+            dst_ref=at(full_ref, owner),
+            send_sem=pass_send.at[k],
+            recv_sem=pass_recv.at[k],
+            device_id={"seq": partner},
+            device_id_type=MESH,
+        )
+
+    barrier = pltpu.get_barrier_semaphore()
+    chips = size // 2
+    for k in range(1, chips):
+        pl.semaphore_signal(barrier, inc=1, device_id={"seq": me ^ (2 * k)}, device_id_type=MESH)
+    pl.semaphore_signal(barrier, inc=1, device_id={"seq": partner}, device_id_type=MESH)
+    pl.semaphore_wait(barrier, chips)
+    for k in range(1, chips):
+        direct(k, me, me ^ (2 * k)).start()
+    direct(0, me, partner).start()
+    own = pltpu.make_async_copy(shard_ref, at(full_ref, me), own_sem)
+    own.start()
+    for k in range(1, chips):
+        direct(k, me ^ (2 * k), me ^ (2 * k)).wait_recv()
+        passed(k, me ^ (2 * k)).start()
+    direct(0, partner, partner).wait_recv()
+    for k in range(1, chips):
+        passed(k, partner ^ (2 * k)).wait_recv()
+    for k in range(chips):
+        direct(k, me, partner).wait_send()
+    for k in range(1, chips):
+        passed(k, me).wait_send()
+    own.wait()
+
+
+def gather(shard):
+    size = lax.axis_size("seq")
+    rows, cols = shard.shape
+    chips = size // 2
+    dma = pltpu.SemaphoreType.DMA
+    return pl.pallas_call(
+        gather_kernel,
+        name="gather",
+        in_specs=[pl.BlockSpec(memory_space=pltpu.VMEM)],
+        out_specs=pl.BlockSpec(memory_space=pl.ANY),
+        out_shape=jax.ShapeDtypeStruct((size * rows, cols), shard.dtype),
+        scratch_shapes=[dma, dma((chips,)), dma((chips,)), dma((chips,)), dma((chips,))],
+        compiler_params=pltpu.CompilerParams(collective_id=0, has_side_effects=True),
+        cost_estimate=pl.CostEstimate(
+            flops=0, bytes_accessed=40 * size * rows * cols, transcendentals=0
+        ),
+    )(shard)
+
+
+def tail_kernel(
+    part_ref,
+    tok_ref,
+    og_ref,
+    gain_ref,
+    wg_ref,
+    vg_ref,
+    small_ref,
+    tg_ref,
+    ws_ref,
+    vs_ref,
+    bc_ref,
+    smallsum_ref,
+    tapsum_ref,
+    gainsum_ref,
+    recv,
+    result,
+    wrecv,
+    vrecv,
+    srecv,
+    grecv,
+    gown,
+    zown,
+    zrecv,
+    town,
+    trecv,
+    rs_send,
+    rs_recv,
+    ag_send,
+    ag_recv,
+    peer_send,
+    peer_recv,
+    own_sem,
+    z_send,
+    z_recv,
+    *,
+    width,
+):
+    pieces, size = part_ref.shape[0], part_ref.shape[1]
+    node = lax.axis_index("head")
+    peers = lax.axis_size("seq")
+    me = lax.axis_index("seq")
+    shard = ws_ref.shape[0]
+    last = size - 1
+    right, left = node + 1, node - 1
+
+    barrier = pltpu.get_barrier_semaphore()
+    for k in range(1, peers):
+        pl.semaphore_signal(barrier, inc=1, device_id={"seq": me ^ k}, device_id_type=MESH)
+    for k in range(1, size):
+        pl.semaphore_signal(
+            barrier, inc=1, device_id={"head": lax.rem(node + k, size)}, device_id_type=MESH
+        )
+    pl.semaphore_wait(barrier, peers + size - 2)
+
+    def slab(ref, owner):
+        return ref.at[pl.ds(pl.multiple_of(owner * shard, 16), shard), :]
+
+    def peer_copies(k, dest, slot):
+        def one(index, src, dst):
+            return pltpu.make_async_remote_copy(
+                src_ref=src,
+                dst_ref=dst,
+                send_sem=peer_send.at[index, k],
+                recv_sem=peer_recv.at[index, k],
+                device_id={"seq": dest},
+                device_id_type=MESH,
+            )
+
+        return (
+            one(0, slab(wg_ref, dest), wrecv.at[slot]),
+            one(1, slab(vg_ref, dest), vrecv.at[slot]),
+            one(2, small_ref, srecv.at[slot]),
+        )
+
+    def gain_copy(k, dest, slot):
+        return pltpu.make_async_remote_copy(
+            src_ref=gown,
+            dst_ref=grecv.at[slot],
+            send_sem=peer_send.at[3, k],
+            recv_sem=peer_recv.at[3, k],
+            device_id={"seq": dest},
+            device_id_type=MESH,
+        )
+
+    def z_copies(k, dest, slot):
+        def one(index, src, dst):
+            return pltpu.make_async_remote_copy(
+                src_ref=src,
+                dst_ref=dst,
+                send_sem=z_send.at[index, k],
+                recv_sem=z_recv.at[index, k],
+                device_id={"head": dest},
+                device_id_type=MESH,
+            )
+
+        return (one(0, zown, zrecv.at[slot]), one(1, town, trecv.at[slot]))
+
+    for k in range(1, peers):
+        for copy in peer_copies(k, me ^ k, k):
+            copy.start()
+    own_w = pltpu.make_async_copy(slab(wg_ref, me), wrecv.at[0], own_sem.at[0])
+    own_v = pltpu.make_async_copy(slab(vg_ref, me), vrecv.at[0], own_sem.at[1])
+    own_w.start()
+    own_v.start()
+    gown[...] = jnp.zeros_like(gown)
+
+    def rs_copy(k, chunk, src, slot, dest):
+        return pltpu.make_async_remote_copy(
+            src_ref=src,
+            dst_ref=recv.at[k, slot],
+            send_sem=rs_send.at[k, chunk],
+            recv_sem=rs_recv.at[k, slot],
+            device_id={"head": dest},
+            device_id_type=MESH,
+        )
+
+    def ag_copy(k, chunk, sem, dest):
+        return pltpu.make_async_remote_copy(
+            src_ref=result.at[k, chunk],
+            dst_ref=result.at[k, chunk],
+            send_sem=ag_send.at[k, sem],
+            recv_sem=ag_recv.at[k, chunk],
+            device_id={"head": dest},
+            device_id_type=MESH,
+        )
+
+    def arrived(k, slot):
+        rs_copy(k, 0, recv.at[k, slot], slot, node).wait_recv()
+
+    def add_own(k, chunk):
+        recv[k, chunk] = (recv[k, chunk].astype(f32) + part_ref[k, chunk].astype(f32)).astype(bf16)
+
+    def reduce_step(k, step):
+        @pl.when((node <= step) & (node < last))
+        def _():
+            chunk = last - step + node
+
+            @pl.when(node > 0)
+            def _():
+                arrived(k, chunk)
+                add_own(k, chunk)
+                rs_copy(k, chunk, recv.at[k, chunk], chunk, right).start()
+
+            @pl.when(node == 0)
+            def _():
+                rs_copy(k, chunk, part_ref.at[k, chunk], chunk, right).start()
+
+        @pl.when((last - node <= step) & (node > 0))
+        def _():
+            chunk = step - (last - node)
+            slot = jnp.where(chunk == node - 1, size, chunk)
+
+            @pl.when(node < last)
+            def _():
+                arrived(k, chunk)
+                add_own(k, chunk)
+                rs_copy(k, chunk, recv.at[k, chunk], slot, left).start()
+
+            @pl.when(node == last)
+            def _():
+                rs_copy(k, chunk, part_ref.at[k, chunk], slot, left).start()
+
+    def emit(k, chunk):
+        hidden = tok_ref[k, chunk].astype(f32)
+        inverse = lax.rsqrt(jnp.mean(hidden * hidden, axis=-1, keepdims=True) + epsilon)
+        unit = hidden * inverse
+        grad = result[k, chunk].astype(f32)
+        both = grad * unit
+        gown[0:1, :] += jnp.sum(both, axis=0, keepdims=True)
+        inner = jnp.mean(both * gain_ref[...], axis=-1, keepdims=True)
+        tg_ref[k, chunk] = (
+            og_ref[k, chunk].astype(f32) + inverse * (grad * gain_ref[...] - unit * inner)
+        ).astype(bf16)
+
+    def own_step(k):
+        @pl.when(node > 0)
+        def _():
+            arrived(k, node)
+
+        @pl.when(node < last)
+        def _():
+            arrived(k, size)
+
+        total = part_ref[k, node].astype(f32)
+        zero = jnp.zeros_like(total)
+        total = total + jnp.where(node > 0, recv[k, node].astype(f32), zero)
+        total = total + jnp.where(node < last, recv[k, size].astype(f32), zero)
+        result[k, node] = total.astype(bf16)
+
+        @pl.when(node < last)
+        def _():
+            ag_copy(k, node, node, right).start()
+
+        @pl.when(node > 0)
+        def _():
+            ag_copy(k, node, size, left).start()
+
+        emit(k, node)
+
+    def pass_step(k, away):
+        @pl.when(node - away >= 0)
+        def _():
+            chunk = node - away
+            ag_copy(k, chunk, chunk, node).wait_recv()
+
+            @pl.when(node < last)
+            def _():
+                ag_copy(k, chunk, chunk, right).start()
+
+            emit(k, chunk)
+
+        @pl.when(node + away <= last)
+        def _():
+            chunk = node + away
+            ag_copy(k, chunk, chunk, node).wait_recv()
+
+            @pl.when(node > 0)
+            def _():
+                ag_copy(k, chunk, chunk, left).start()
+
+            emit(k, chunk)
+
+    def finish_weights():
+        for k in range(1, peers):
+            for copy in peer_copies(k, me ^ k, k):
+                copy.wait_recv()
+        own_w.wait()
+        own_v.wait()
+
+        def rows(step, carry):
+            here = pl.ds(pl.multiple_of(step * 16, 16), 16)
+            total = wrecv[0, here, :].astype(f32)
+            other = vrecv[0, here, :].astype(f32)
+            for k in range(1, peers):
+                total = total + wrecv[k, here, :].astype(f32)
+                other = other + vrecv[k, here, :].astype(f32)
+            ws_ref[here, :] = total
+            vs_ref[here, :] = other
+            zown[here, :] = total[:, 2 * width : 2 * width + 2 * NST].astype(bf16)
+            return carry
+
+        lax.fori_loop(0, shard // 16, rows, 0)
+        total = small_ref[...]
+        for k in range(1, peers):
+            total = total + srecv[k]
+        smallsum_ref[...] = total
+        town[...] = total[0:EDGE, width:]
+        for k in range(1, size):
+            for copy in z_copies(k, lax.rem(node + k, size), k):
+                copy.start()
+
+    steps = 2 * last
+
+    def tick(t, carry):
+        for s in range(steps + 1):
+            k = t - s
+
+            @pl.when((k >= 0) & (k < pieces))
+            def _():
+                if s < last:
+                    reduce_step(k, s)
+                elif s == last:
+                    own_step(k)
+                else:
+                    pass_step(k, s - last)
+
+        @pl.when(t == pieces)
+        def _():
+            finish_weights()
+
+        return carry
+
+    lax.fori_loop(0, pieces + steps, tick, 0)
+
+    for k in range(1, peers):
+        gain_copy(k, me ^ k, k).start()
+    for k in range(1, size):
+        for copy in z_copies(k, node, k):
+            copy.wait_recv()
+    total = zown[...].astype(f32)
+    taps = town[...]
+    for k in range(1, size):
+        total = total + zrecv[k].astype(f32)
+        taps = taps + trecv[k]
+    bc_ref[...] = total
+    tapsum_ref[...] = taps
+    for k in range(1, peers):
+        gain_copy(k, me ^ k, k).wait_recv()
+    gain = gown[...]
+    for k in range(1, peers):
+        gain = gain + grecv[k]
+    gainsum_ref[...] = gain
+
+    def drain(k, carry):
+        for chunk in range(size):
+
+            @pl.when(chunk != node)
+            def _():
+                rs_copy(k, chunk, recv.at[k, chunk], chunk, node).wait_send()
+
+            @pl.when((chunk < node) & (node < last) | (chunk > node) & (node > 0))
+            def _():
+                ag_copy(k, chunk, chunk, node).wait_send()
+
+        @pl.when(node < last)
+        def _():
+            ag_copy(k, node, node, node).wait_send()
+
+        @pl.when(node > 0)
+        def _():
+            ag_copy(k, node, size, node).wait_send()
+
+        return carry
+
+    lax.fori_loop(0, pieces, drain, 0)
+    for k in range(1, peers):
+        for copy in peer_copies(k, me ^ k, k):
+            copy.wait_send()
+        gain_copy(k, me ^ k, k).wait_send()
+    for k in range(1, size):
+        for copy in z_copies(k, node, k):
+            copy.wait_send()
+
+
+def tail(part, tokens, grads, gain, wg, vg, small, width):
+    pieces, size, rows, model = part.shape
+    peers = lax.axis_size("seq")
+    shard = wg.shape[0] // peers
+    cols, wide = wg.shape[1], small.shape[1]
+    dma = pltpu.SemaphoreType.DMA
+    vmem = pl.BlockSpec(memory_space=pltpu.VMEM)
+    hbm = pl.BlockSpec(memory_space=pl.ANY)
+    return pl.pallas_call(
+        functools.partial(tail_kernel, width=width),
+        name="tail",
+        in_specs=[vmem, vmem, vmem, vmem, hbm, hbm, vmem],
+        out_specs=[vmem] * 7,
+        out_shape=[
+            spec(pieces, size, rows, model, dtype=bf16),
+            spec(shard, cols),
+            spec(shard, width),
+            spec(shard, 2 * NST),
+            spec(*small.shape),
+            spec(EDGE, 2 * NST),
+            spec(EDGE, model),
+        ],
+        scratch_shapes=[
+            pltpu.VMEM((pieces, size + 1, rows, model), bf16),
+            pltpu.VMEM((pieces, size, rows, model), bf16),
+            pltpu.VMEM((peers, shard, cols), bf16),
+            pltpu.VMEM((peers, shard, width), bf16),
+            pltpu.VMEM((peers,) + small.shape, f32),
+            pltpu.VMEM((peers, EDGE, model), f32),
+            pltpu.VMEM((EDGE, model), f32),
+            pltpu.VMEM((shard, 2 * NST), bf16),
+            pltpu.VMEM((size, shard, 2 * NST), bf16),
+            pltpu.VMEM((EDGE, 2 * NST), f32),
+            pltpu.VMEM((size, EDGE, 2 * NST), f32),
+            dma((pieces, size)),
+            dma((pieces, size + 1)),
+            dma((pieces, size + 1)),
+            dma((pieces, size)),
+            dma((4, peers)),
+            dma((4, peers)),
+            dma((2,)),
+            dma((2, size)),
+            dma((2, size)),
+        ],
+        compiler_params=pltpu.CompilerParams(
+            collective_id=1, has_side_effects=True, vmem_limit_bytes=63 * 1024 * 1024
+        ),
+        cost_estimate=pl.CostEstimate(
+            flops=0, bytes_accessed=60 * part.size, transcendentals=0
+        ),
+    )(part, tokens, grads, gain, wg, vg, small)
+
+
+def sum_over_heads(value):
+    size = lax.axis_size("head")
+    total = value
+    for k in range(1, size):
+        total = total + lax.ppermute(value, "head", [(i, (i + k) % size) for i in range(size)])
+    return total
+
+
 def local(
     tokens,
     norm_gain,
@@ -581,8 +1043,8 @@
     w_shard = jnp.concatenate(
         [w_z, w_x, w_bc, w_dt, jnp.zeros((w_dt.shape[0], LANES - heads), bf16)], axis=1
     )
-    w_all = lax.all_gather(w_shard, "seq", axis=0, tiled=True)
-    w_back = lax.all_gather(w_out, "seq", axis=1, tiled=True)
+    w_all = gather(w_shard)
+    w_back = lax.all_gather(w_out.T, "seq", axis=0, tiled=True)
 
     positions = lax.axis_index("seq") * rows + jnp.arange(rows, dtype=jnp.int32)
     valid = positions[None, :] < lengths.reshape(batch)[:, None]
@@ -665,7 +1127,7 @@
                 2 * per * rows * model * width,
             )
         )
-    sums = [lax.psum(second[g][2], "head") for g in range(GROUPS)]
+    sums = [sum_over_heads(second[g][2]) for g in range(GROUPS)]
 
     third = []
     for g in range(GROUPS):
@@ -753,7 +1215,6 @@
                 2 * per * rows * model * w_all.shape[1],
             )
         )
-    summed = [lax.psum(fifth[g][1], "head") for g in range(GROUPS)]
 
     def joined(parts):
         return jnp.concatenate(parts, axis=0).reshape(batch * rows, -1)
@@ -766,14 +1227,35 @@
     w_grad = jnp.concatenate(
         [mm(normed, gz, TN), mm(normed, gj, TN), mm(normed, gdt, TN)], axis=1
     ).astype(bf16)
-    out_w_grad = mm(gnorm, grad_branch.reshape(batch * rows, model), TN).astype(bf16)
-    w_sum = lax.psum_scatter(w_grad, "seq", scatter_dimension=0, tiled=True)
-    out_w_sum = lax.psum_scatter(out_w_grad, "seq", scatter_dimension=1, tiled=True)
-    bc_sum = lax.psum(w_sum[:, 2 * width : 2 * width + 2 * NST], "head")
+    out_w_grad = mm(grad_branch.reshape(batch * rows, model), gnorm, TN).astype(bf16)
+
+    cols = sum(jnp.sum(t[8], axis=0) for t in third)
+    tap_sum = sum(jnp.sum(t[3], axis=0) for t in fourth)
+    head_sum = sum(jnp.sum(t[4], axis=0) for t in fourth)
+    small = jnp.concatenate(
+        [
+            tap_sum,
+            jnp.concatenate([cols, jnp.zeros((EDGE, wide - width), f32)], axis=1),
+            jnp.concatenate([head_sum, jnp.zeros((EDGE, wide - LANES), f32)], axis=1),
+        ],
+        axis=0,
+    )
+    head_size = lax.axis_size("head")
+    cut = (PIECES, head_size, batch * rows // (PIECES * head_size), model)
+    partial_in = jnp.concatenate([t[1] for t in fifth], axis=0)
+    input_grads, w_sum, out_w_sum, bc_sum, small, bc_taps, gain_grad = tail(
+        partial_in.reshape(cut),
+        flat.reshape(cut),
+        flat_grad.reshape(cut),
+        norm_gain[None],
+        w_grad,
+        out_w_grad,
+        small,
+        width,
+    )
+    skip = jnp.sum(small[EDGE + 1, :width].reshape(heads, HEAD_DIM), axis=1)
 
     layer_outs = []
-    input_grads = []
-    gain_grad = jnp.zeros((model,), f32)
     for g in range(GROUPS):
         part = slice(g * per, (g + 1) * per)
         hidden = flat[part].astype(f32)
@@ -782,45 +1264,25 @@
                 valid[part][:, :, None], hidden + branches[g].astype(f32), hidden
             ).astype(bf16)
         )
-        inverse = lax.rsqrt(jnp.mean(hidden * hidden, axis=-1, keepdims=True) + epsilon)
-        unit = hidden * inverse
-        grad_in = summed[g].astype(f32)
-        gain_grad = gain_grad + jnp.sum(grad_in * unit, axis=(0, 1))
-        scaled = grad_in * norm_gain
-        input_grads.append(
-            (
-                flat_grad[part].astype(f32)
-                + inverse * (scaled - unit * jnp.mean(scaled * unit, axis=-1, keepdims=True))
-            ).astype(bf16)
-        )
-
-    cols = sum(jnp.sum(t[8], axis=0) for t in third)
-    tap_sum = sum(jnp.sum(t[3], axis=0) for t in fourth)
-    head_sum = sum(jnp.sum(t[4], axis=0) for t in fourth)
-    skip = jnp.sum(cols[1].reshape(heads, HEAD_DIM), axis=1)
-    gain_grad, cols0, tap_sum, head_sum, skip = lax.psum(
-        (gain_grad, cols[0], tap_sum[: CONV + 1], head_sum[:2], skip), "seq"
-    )
-    bc_taps = lax.psum(tap_sum[:, width:], "head")
 
     out_shape = (micro, seqs, rows, model)
     return (
         jnp.concatenate(layer_outs, axis=0).reshape(out_shape),
-        jnp.concatenate(input_grads, axis=0).reshape(out_shape),
-        gain_grad,
-        w_sum[:, :width].astype(f32),
-        w_sum[:, width : 2 * width].astype(f32),
-        bc_sum.astype(f32),
-        w_sum[:, 2 * width + 2 * NST : 2 * width + 2 * NST + heads].astype(f32),
-        tap_sum[:CONV, :width],
-        tap_sum[CONV, :width],
+        input_grads.reshape(out_shape),
+        gain_grad[0],
+        w_sum[:, :width],
+        w_sum[:, width : 2 * width],
+        bc_sum,
+        w_sum[:, 2 * width + 2 * NST : 2 * width + 2 * NST + heads],
+        small[:CONV, :width],
+        small[CONV, :width],
         bc_taps[:CONV],
         bc_taps[CONV],
-        head_sum[0, :heads],
-        head_sum[1, :heads],
+        small[2 * EDGE, :heads],
+        small[2 * EDGE + 1, :heads],
         skip,
-        cols0,
-        out_w_sum.astype(f32),
+        small[EDGE, :width],
+        out_w_sum.T,
     )
 
 

time: 1120 us -> 842 us (0.75)
  waiting for transfers between devices: 645 us -> 62.9 us
  Pallas kernels: 236 us -> 581 us
  blocking collectives: 34.9 us -> 0 us
  other arithmetic: 63.9 us -> 47.6 us
  starting transfers between devices: 28.6 us -> 44.9 us
    psum x2 -> x1, waiting for transfers between devices: 468 us -> 0.01 us  [local(): branches = [lax.psum(third[g][1], 'head') for g in range(GROUPS)]]
    pallas_call x0 -> x2, Pallas kernels: none -> 345 us  [the longest x1 296 us: tail(): pl.pallas_call(functools.partial(tail_kernel, width=width), name='tail',...]
    unnamed x7 -> x2, waiting for transfers between devices: 50.3 us -> 0.03 us
    all_gather x2 -> x1, waiting for transfers between devices: 49.5 us -> 0.01 us  [local(): w_back = lax.all_gather(w_out.T, 'seq', axis=0, tiled=True)]
    reduce_scatter x1 -> x0, waiting for transfers between devices: 40.8 us -> none  [local(): lax.psum_scatter(out_w_grad, 'seq', scatter_dimension=1, tiled=True)]
    psum x2 -> x0, blocking collectives: 34.9 us -> none  [the longest x1 25.1 us: local(): lax.psum((gain_grad, cols[0], tap_sum[:CONV + 1], head_sum[:2], skip), 's...]
    ppermute x24, waiting for transfers between devices: 36 us -> 56.5 us  [exchange(): got = lax.ppermute(payload, axis, [(i, i ^ bit) for i in range(size)])]
    ppermute x0 -> x12, starting transfers between devices: none -> 17.9 us  [sum_over_heads(): lax.ppermute(value, 'head', [(i, (i + k) % size) for i in range(size)])]
  transfers between devices with their start and end apart: 35 -> 43, of which waited for: 13 -> 17; matrix products, arithmetic and copies ran while one was open for 8% -> 12% of each run, Pallas kernels for 16% -> 67%
where the time goes in v2:
time: 842 us; the launch traced here: 832 us
  Pallas kernels  581 us (69%)
  waiting for transfers between devices  62.9 us (7%)
  local copies, waits for them, and re-layouts  48.7 us (6%)
  other arithmetic  47.6 us (6%)
  starting transfers between devices  44.9 us (5%)
  matrix products  31.1 us (4%)
  between operations  15.9 us (2%)
    pallas_call x1, Pallas kernels, tail(): pl.pallas_call(functools.partial(tail_kernel, width=width), name='tail',...  296 us
    pallas_call x20, Pallas kernels, run(): pl.pallas_call(body, name=name, grid=(count,), in_specs=[per_sequence(a.s...  236 us
    ppermute x24, waiting for transfers between devices, exchange(): got = lax.ppermute(payload, axis, [(i, i ^ bit) for i in range(size)])  56.5 us
    pallas_call x1, Pallas kernels, gather(): pl.pallas_call(gather_kernel, name='gather', in_specs=[pl.BlockSpec(memor...  49.1 us
    dot_general x4, matrix products, mm(): return lax.dot_general(a, b, dims, preferred_element_type=f32)  31.1 us
    ppermute x24, starting transfers between devices, exchange(): got = lax.ppermute(payload, axis, [(i, i ^ bit) for i in range(size)])  19.2 us
    ppermute x12, starting transfers between devices, sum_over_heads(): lax.ppermute(value, 'head', [(i, (i + k) % size) for i in range(size)])  17.9 us
  transfers between devices with their start and end apart: 43, of which 17 were waited for; matrix products, arithmetic and copies ran while one was open for 12% of the time, Pallas kernels for 67%

profile of v2, /device:TPU:0, one launch (start us, length us, event | category | flops | bytes accessed | tf_op | source)
XLA Modules:
  0.0 832.2 jit_solution(7273203610121276555)
XLA Ops:
  18.5 49.1 %gather.1.w_ref = bf16[1536,1920]{1,0:T(8,128)(2,1)} custom-call(bf16[192,1920]{1,0:T(8,128)(2,1)} %concatenate.118.shard_ref), custom_call_target="tpu_custom_call" | custom-call | bytes 117964800 | tf_op jit(solution)/shard_map/gather/pallas_call | solution.py:607
  79.4 15.0 %project.4 = (bf16[1,512,1536]{2,1,0:T(8,128)(2,1)}, bf16[1,512,1792]{2,1,0:T(8,128)(2,1)}, f32[1,512,128]{2,1,0:T(8,128)}, bf16[1,512,1024]{2,1,0:T(8,128)(2,1)...) custom-call(bf16[1,512,1536]{2,1,0:T(8,128)(2,1)} %get-tuple-element, ...), custom_call_target="tpu_custom_call" | custom-call | flops 3019898880 | bytes 14567424 | tf_op jit(solution)/shard_map/project/pallas_call | solution.py:500
  96.3 14.9 %project.7 = (bf16[1,512,1536]{2,1,0:T(8,128)(2,1)}, bf16[1,512,1792]{2,1,0:T(8,128)(2,1)}, f32[1,512,128]{2,1,0:T(8,128)}, bf16[1,512,1024]{2,1,0:T(8,128)(2,1)...) custom-call(bf16[1,512,1536]{2,1,0:T(8,128)(2,1)} %get-tuple-element, ...), custom_call_target="tpu_custom_call" | custom-call | flops 3019898880 | bytes 14567424 | tf_op jit(solution)/shard_map/project/pallas_call | solution.py:500
  112.1 15.0 %project.6 = (bf16[1,512,1536]{2,1,0:T(8,128)(2,1)}, bf16[1,512,1792]{2,1,0:T(8,128)(2,1)}, f32[1,512,128]{2,1,0:T(8,128)}, bf16[1,512,1024]{2,1,0:T(8,128)(2,1)...) custom-call(bf16[1,512,1536]{2,1,0:T(8,128)(2,1)} %get-tuple-element, ...), custom_call_target="tpu_custom_call" | custom-call | flops 3019898880 | bytes 14567424 | tf_op jit(solution)/shard_map/project/pallas_call | solution.py:500
  128.2 15.0 %project.5 = (bf16[1,512,1536]{2,1,0:T(8,128)(2,1)}, bf16[1,512,1792]{2,1,0:T(8,128)(2,1)}, f32[1,512,128]{2,1,0:T(8,128)}, bf16[1,512,1024]{2,1,0:T(8,128)(2,1)...) custom-call(bf16[1,512,1536]{2,1,0:T(8,128)(2,1)} %get-tuple-element, ...), custom_call_target="tpu_custom_call" | custom-call | flops 3019898880 | bytes 14567424 | tf_op jit(solution)/shard_map/project/pallas_call | solution.py:500
  171.3 7.8 gate.4
  188.2 15.8 %mixer.4 = (bf16[1,512,768]{2,1,0:T(8,128)(2,1)}, bf16[1,512,1536]{2,1,0:T(8,128)(2,1)}, bf16[1,512,768]{2,1,0:T(8,128)(2,1)}, bf16[1,512,768]{2,1,0:T(8,128)(2,...) custom-call(f32[1,8,512]{2,1,0:T(8,128)} %add_add_fusion.3.sums_ref,, ...), custom_call_target="tpu_custom_call" | custom-call | flops 1207959552 | bytes 12718080 | tf_op jit(solution)/shard_map/mixer/pallas_call | solution.py:500
  234.1 11.4 %conv.4 = (bf16[1,512,1024]{2,1,0:T(8,128)(2,1)}, bf16[1,512,128]{2,1,0:T(8,128)(2,1)}, f32[1,8,1024]{2,1,0:T(8,128)}, f32[1,8,1024]{2,1,0:T(8,128)}, f32[1,8,128]{2,1,0:T(8,128)}) custom-call(bf16[1,512,1792]{2,1,0:T(8,128)(2,1)} %get-tuple-element.138.proj_ref, f32[1,8,1024]{2,1,0:T(8,128)} %get-tuple-element.180.edge_ref, ...), custom_call_target="tpu_custom_call" | custom-call | flops 31457280 | bytes 7151616 | tf_op jit(solution)/shard_map/conv/pallas_call | solution.py:500
  248.0 7.6 gate.5
  264.7 16.0 %mixer.5 = (bf16[1,512,768]{2,1,0:T(8,128)(2,1)}, bf16[1,512,1536]{2,1,0:T(8,128)(2,1)}, bf16[1,512,768]{2,1,0:T(8,128)(2,1)}, bf16[1,512,768]{2,1,0:T(8,128)(2,...) custom-call(f32[1,8,512]{2,1,0:T(8,128)} %add_add_fusion.2.sums_ref,, ...), custom_call_target="tpu_custom_call" | custom-call | flops 1207959552 | bytes 12718080 | tf_op jit(solution)/shard_map/mixer/pallas_call | solution.py:500
  286.5 8.9 %input_grad.4 = (bf16[1,512,1024]{2,1,0:T(8,128)(2,1)}, bf16[1,512,1536]{2,1,0:T(8,128)(2,1)}) custom-call(bf16[1,512,768]{2,1,0:T(8,128)(2,1)} %get-tuple-element.179.gz_ref, bf16[1,512,1024]{2,1,0:T(8,128)(2,1)} %get-tuple-element.186.gj_ref, bf16[1,512,128]{2,1,0:T(8,128)(2,1)} %get-tuple-element.187.gdt_ref, f32[1,8,1024]{2,1,0:T(8,128)} %copy-done.54, ...), custom_call_target="tpu_custom_call" | custom-call | flops 3019898880 | bytes 10551296 | tf_op jit(solution)/shard_map/input_grad/pallas_call | solution.py:500
  299.2 9.7 %collective-permute-done.15 = bf16[1,144,768]{2,1,0:T(8,128)(2,1)S(1)} collective-permute-done((bf16[1,144,768]{2,1,0:T(8,128)(2,1)S(1)}, bf16[1,144,768]{2,1,0:T(8,128)(2,1)S(1)}, u32[]{:S(2)}, u32[]{:S(2)}) %collective-permute-start.15) | collective-permute-done | bytes 221216 | tf_op jit(solution)/shard_map/ppermute | solution.py:527
  309.8 7.6 gate.6
  332.6 11.9 %conv.5 = (bf16[1,512,1024]{2,1,0:T(8,128)(2,1)}, bf16[1,512,128]{2,1,0:T(8,128)(2,1)}, f32[1,8,1024]{2,1,0:T(8,128)}, f32[1,8,1024]{2,1,0:T(8,128)}, f32[1,8,128]{2,1,0:T(8,128)}) custom-call(bf16[1,512,1792]{2,1,0:T(8,128)(2,1)} %get-tuple-element.149.proj_ref, f32[1,8,1024]{2,1,0:T(8,128)} %get-tuple-element.191.edge_ref, ...), custom_call_target="tpu_custom_call" | custom-call | flops 31457280 | bytes 7151616 | tf_op jit(solution)/shard_map/conv/pallas_call | solution.py:500
  349.3 15.8 %mixer.6 = (bf16[1,512,768]{2,1,0:T(8,128)(2,1)}, bf16[1,512,1536]{2,1,0:T(8,128)(2,1)}, bf16[1,512,768]{2,1,0:T(8,128)(2,1)}, bf16[1,512,768]{2,1,0:T(8,128)(2,...) custom-call(f32[1,8,512]{2,1,0:T(8,128)} %add_add_fusion.1.sums_ref,, ...), custom_call_target="tpu_custom_call" | custom-call | flops 1207959552 | bytes 12718080 | tf_op jit(solution)/shard_map/mixer/pallas_call | solution.py:500
  367.8 15.9 %mixer.7 = (bf16[1,512,768]{2,1,0:T(8,128)(2,1)}, bf16[1,512,1536]{2,1,0:T(8,128)(2,1)}, bf16[1,512,768]{2,1,0:T(8,128)(2,1)}, bf16[1,512,768]{2,1,0:T(8,128)(2,...) custom-call(f32[1,8,512]{2,1,0:T(8,128)} %add_add_fusion.sums_ref, ...), custom_call_target="tpu_custom_call" | custom-call | flops 1207959552 | bytes 12718080 | tf_op jit(solution)/shard_map/mixer/pallas_call | solution.py:500
  384.9 8.7 %bitcast_convert_fusion.1.vg_ref = bf16[1536,768]{1,0:T(8,128)(2,1)} fusion(bf16[4,512,1536]{2,1,0:T(8,128)(2,1)} %copy-done, bf16[1,512,768]{2,1,0:T(8,128)(2,1)} %get-tuple-element.234, bf16[1,512,768]{2,1,0:T(8,128)(2,1)S(1)} %copy-done.50, bf16[1,512,768]{2,1,0:T(8,128)(2,1)S(1)} %copy-done.47, bf16[1,512,768]{2,1,0:T(8,128)(2,1)S(1)} %copy-done.45), kind=kOutput, calls=%fused_computation.9 | convolution fusion | flops 4837736448 | bytes 11796480 | tf_op jit(solution)/shard_map/dot_general | solution.py:29
  401.8 9.1 %input_grad.5 = (bf16[1,512,1024]{2,1,0:T(8,128)(2,1)}, bf16[1,512,1536]{2,1,0:T(8,128)(2,1)}) custom-call(bf16[1,512,768]{2,1,0:T(8,128)(2,1)} %get-tuple-element.190.gz_ref, bf16[1,512,1024]{2,1,0:T(8,128)(2,1)} %get-tuple-element.197.gj_ref, bf16[1,512,128]{2,1,0:T(8,128)(2,1)} %get-tuple-element.198.gdt_ref, f32[1,8,1024]{2,1,0:T(8,128)} %copy-done.55, ...), custom_call_target="tpu_custom_call" | custom-call | flops 3019898880 | bytes 10551296 | tf_op jit(solution)/shard_map/input_grad/pallas_call | solution.py:500
  428.4 11.4 %conv.6 = (bf16[1,512,1024]{2,1,0:T(8,128)(2,1)}, bf16[1,512,128]{2,1,0:T(8,128)(2,1)}, f32[1,8,1024]{2,1,0:T(8,128)}, f32[1,8,1024]{2,1,0:T(8,128)}, f32[1,8,128]{2,1,0:T(8,128)}) custom-call(bf16[1,512,1792]{2,1,0:T(8,128)(2,1)} %get-tuple-element.160.proj_ref, f32[1,8,1024]{2,1,0:T(8,128)} %get-tuple-element.202.edge_ref, ...), custom_call_target="tpu_custom_call" | custom-call | flops 31457280 | bytes 7151616 | tf_op jit(solution)/shard_map/conv/pallas_call | solution.py:500
  444.2 8.9 %input_grad.6 = (bf16[1,512,1024]{2,1,0:T(8,128)(2,1)}, bf16[1,512,1536]{2,1,0:T(8,128)(2,1)}) custom-call(bf16[1,512,768]{2,1,0:T(8,128)(2,1)} %get-tuple-element.201.gz_ref, bf16[1,512,1024]{2,1,0:T(8,128)(2,1)} %get-tuple-element.208.gj_ref, bf16[1,512,128]{2,1,0:T(8,128)(2,1)} %get-tuple-element.209.gdt_ref, f32[1,8,1024]{2,1,0:T(8,128)} %copy-done.57, ...), custom_call_target="tpu_custom_call" | custom-call | flops 3019898880 | bytes 10551296 | tf_op jit(solution)/shard_map/input_grad/pallas_call | solution.py:500
  453.9 11.5 %conv.7 = (bf16[1,512,1024]{2,1,0:T(8,128)(2,1)}, bf16[1,512,128]{2,1,0:T(8,128)(2,1)}, f32[1,8,1024]{2,1,0:T(8,128)}, f32[1,8,1024]{2,1,0:T(8,128)}, f32[1,8,128]{2,1,0:T(8,128)}) custom-call(bf16[1,512,1792]{2,1,0:T(8,128)(2,1)} %get-tuple-element.171.proj_ref, f32[1,8,1024]{2,1,0:T(8,128)} %get-tuple-element.213.edge_ref, ...), custom_call_target="tpu_custom_call" | custom-call | flops 31457280 | bytes 7151616 | tf_op jit(solution)/shard_map/conv/pallas_call | solution.py:500
  474.2 8.8 %input_grad.7 = (bf16[1,512,1024]{2,1,0:T(8,128)(2,1)}, bf16[1,512,1536]{2,1,0:T(8,128)(2,1)}) custom-call(bf16[1,512,768]{2,1,0:T(8,128)(2,1)} %get-tuple-element.212.gz_ref, bf16[1,512,1024]{2,1,0:T(8,128)(2,1)} %get-tuple-element.219.gj_ref, bf16[1,512,128]{2,1,0:T(8,128)(2,1)} %get-tuple-element.220.gdt_ref, f32[1,8,1024]{2,1,0:T(8,128)} %copy-done.56, ...), custom_call_target="tpu_custom_call" | custom-call | flops 3019898880 | bytes 10551296 | tf_op jit(solution)/shard_map/input_grad/pallas_call | solution.py:500
  483.1 10.4 %bitcast_convert_fusion = bf16[1536,1024]{1,0:T(8,128)(2,1)S(1)} fusion(bf16[4,512,1536]{2,1,0:T(8,128)(2,1)} %copy-done.17, bf16[1,512,1024]{2,1,0:T(8,128)(2,1)} %get-tuple-element.230, bf16[1,512,1024]{2,1,0:T(8,128)(2,1)} %get-tuple-element.229, bf16[1,512,1024]{2,1,0:T(8,128)(2,1)} %get-tuple-element.228, bf16[1,512,1024]{2,1,0:T(8,128)(2,1)} %get-tuple-element.227), kind=kOutput, calls=%fused_computation.2 | convolution fusion | flops 6450315264 | bytes 13631488 | tf_op jit(solution)/shard_map/dot_general | solution.py:29
  501.6 295.8 %tail.1 = (bf16[8,4,64,1536]{3,2,1,0:T(8,128)(2,1)}, f32[192,1920]{1,0:T(8,128)}, f32[192,768]{1,0:T(8,128)}, f32[192,256]{1,0:T(8,128)}, f32[24,1024]{1,0:T(8,1...) custom-call(bf16[8,4,64,1536]{3,2,1,0:T(8,128)(2,1)} %bitcast.44, bf16[8,4,64,1536]{3,2,1,0:T(8,128)(2,1)} %bitcast.42, ...), custom_call_target="tpu_custom_call" | custom-call | bytes 188743680 | tf_op jit(solution)/shard_map/tail/pallas_call | solution.py:954
  (388 shorter events, 214.1 us)
Async XLA Ops:
  7.2 164.1 %all-gather.2.cloned.1.call-start = ((), (), s32[]{:S(2)}) async-start(), calls=%async_computation | async-start | bytes 2654208 | tf_op jit(solution)/shard_map/all_gather | solution.py:1047
  8.2 70.5 %collective-permute-start = (bf16[4,16,1536]{2,1,0:T(8,128)(2,1)S(1)}, bf16[4,16,1536]{2,1,0:T(8,128)(2,1)S(1)}, u32[]{:S(2)}, u32[]{:S(2)}) collective-permute-start(bf16[4,16,1536]{2,1,0:T(8,128)(2,1)S(1)} %slice.358), channel_id=1, source_target_pairs={{0,4},{4,8},{8,12},{12,16},{16,20},{20,24},{24,28},{1,5},{5,9},{9,... | collective-permute-start | bytes 589832 | tf_op jit(solution)/shard_map/ppermute | solution.py:1037
  10.6 799.4 %all-reduce.7.cloned.1.call-start = ((), (), s32[]{:S(2)}) async-start(), calls=%async_computation.1 | async-start | bytes 12582912 | tf_op jit(solution)/shard_map/psum | solution.py:1168
  94.4 60.3 %collective-permute-start.1 = (bf16[1,144,768]{2,1,0:T(8,128)(2,1)}, bf16[1,144,768]{2,1,0:T(8,128)(2,1)S(1)}, u32[]{:S(2)}, u32[]{:S(2)}) collective-permute-start(bf16[1,144,768]{2,1,0:T(8,128)(2,1)} %get-tuple-element.139), channel_id=1, source_target_pairs={{0,4},{4,0},{8,12},{12,8},{16,20},{20,16},{24,28},{28,24},{1,5},{5... | collective-permute-start | bytes 663560 | tf_op jit(solution)/shard_map/ppermute | solution.py:527
  111.2 45.0 %collective-permute-start.19 = (bf16[1,144,768]{2,1,0:T(8,128)(2,1)}, bf16[1,144,768]{2,1,0:T(8,128)(2,1)S(1)}, u32[]{:S(2)}, u32[]{:S(2)}) collective-permute-start(bf16[1,144,768]{2,1,0:T(8,128)(2,1)} %get-tuple-element.172), channel_id=1, source_target_pairs={{0,4},{4,0},{8,12},{12,8},{16,20},{20,16},{24,28},{28,24},{1,5},{5... | collective-permute-start | bytes 663560 | tf_op jit(solution)/shard_map/ppermute | solution.py:527
  127.1 29.0 %collective-permute-start.13 = (bf16[1,144,768]{2,1,0:T(8,128)(2,1)}, bf16[1,144,768]{2,1,0:T(8,128)(2,1)S(1)}, u32[]{:S(2)}, u32[]{:S(2)}) collective-permute-start(bf16[1,144,768]{2,1,0:T(8,128)(2,1)} %get-tuple-element.161), channel_id=1, source_target_pairs={{0,4},{4,0},{8,12},{12,8},{16,20},{20,16},{24,28},{28,24},{1,5},{5... | collective-permute-start | bytes 663560 | tf_op jit(solution)/shard_map/ppermute | solution.py:527
  143.2 12.9 %collective-permute-start.7 = (bf16[1,144,768]{2,1,0:T(8,128)(2,1)}, bf16[1,144,768]{2,1,0:T(8,128)(2,1)S(1)}, u32[]{:S(2)}, u32[]{:S(2)}) collective-permute-start(bf16[1,144,768]{2,1,0:T(8,128)(2,1)} %get-tuple-element.150), channel_id=1, source_target_pairs={{0,4},{4,0},{8,12},{12,8},{16,20},{20,16},{24,28},{28,24},{1,5},{5... | collective-permute-start | bytes 663560 | tf_op jit(solution)/shard_map/ppermute | solution.py:527
  216.7 16.6 %collective-permute-start.27 = (bf16[1,144,768]{2,1,0:T(8,128)(2,1)S(1)}, bf16[1,144,768]{2,1,0:T(8,128)(2,1)S(1)}, u32[]{:S(2)}, u32[]{:S(2)}) collective-permute-start(bf16[1,144,768]{2,1,0:T(8,128)(2,1)S(1)} %get-tuple-element.333), channel_id=1, source_target_pairs={{0,16},{4,20},{8,24},{12,28},{16,0},{20,4},{24,8},{28,12},{1,17},{... | collective-permute-start | bytes 663560 | tf_op jit(solution)/shard_map/ppermute | solution.py:527
  218.2 12.3 %collective-permute-start.20 = (bf16[1,144,768]{2,1,0:T(8,128)(2,1)S(1)}, bf16[1,144,768]{2,1,0:T(8,128)(2,1)S(1)}, u32[]{:S(2)}, u32[]{:S(2)}) collective-permute-start(bf16[1,144,768]{2,1,0:T(8,128)(2,1)S(1)} %get-tuple-element.336), channel_id=1, source_target_pairs={{0,8},{4,12},{8,0},{12,4},{16,24},{20,28},{24,16},{28,20},{1,9},{5... | collective-permute-start | bytes 663560 | tf_op jit(solution)/shard_map/ppermute | solution.py:527
  219.4 13.8 %collective-permute-start.14 = (bf16[1,144,768]{2,1,0:T(8,128)(2,1)S(1)}, bf16[1,144,768]{2,1,0:T(8,128)(2,1)S(1)}, u32[]{:S(2)}, u32[]{:S(2)}) collective-permute-start(bf16[1,144,768]{2,1,0:T(8,128)(2,1)S(1)} %get-tuple-element.335), channel_id=1, source_target_pairs={{0,8},{4,12},{8,0},{12,4},{16,24},{20,28},{24,16},{28,20},{1,9},{5... | collective-permute-start | bytes 663560 | tf_op jit(solution)/shard_map/ppermute | solution.py:527
  226.1 21.1 %collective-permute-start.9 = (bf16[1,144,768]{2,1,0:T(8,128)(2,1)S(1)}, bf16[1,144,768]{2,1,0:T(8,128)(2,1)S(1)}, u32[]{:S(2)}, u32[]{:S(2)}) collective-permute-start(bf16[1,144,768]{2,1,0:T(8,128)(2,1)S(1)} %maximum_maximum_fusion.3), channel_id=1, source_target_pairs={{0,16},{4,20},{8,24},{12,28},{16,0},{20,4},{24,8},{28,12},{1,17},{... | collective-permute-start | bytes 663560 | tf_op jit(solution)/shard_map/ppermute | solution.py:527
  245.5 40.4 %collective-permute-start.28 = (f32[1,8,1024]{2,1,0:T(8,128)}, f32[1,8,1024]{2,1,0:T(8,128)S(1)}, u32[]{:S(2)}, u32[]{:S(2)}) collective-permute-start(f32[1,8,1024]{2,1,0:T(8,128)} %get-tuple-element.188), channel_id=1, source_target_pairs={{4,0},{8,4},{12,8},{16,12},{20,16},{24,20},{28,24},{5,1},{9,5},{13... | collective-permute-start | bytes 98312 | tf_op jit(solution)/shard_map/ppermute | solution.py:1199
  295.8 34.5 %collective-permute-start.31 = (bf16[1,144,768]{2,1,0:T(8,128)(2,1)S(1)}, bf16[1,144,768]{2,1,0:T(8,128)(2,1)S(1)}, u32[]{:S(2)}, u32[]{:S(2)}) collective-permute-start(bf16[1,144,768]{2,1,0:T(8,128)(2,1)S(1)} %get-tuple-element.337), channel_id=1, source_target_pairs={{0,16},{4,20},{8,24},{12,28},{16,0},{20,4},{24,8},{28,12},{1,17},{... | collective-permute-start | bytes 663560 | tf_op jit(solution)/shard_map/ppermute | solution.py:527
  297.2 11.7 %collective-permute-start.15 = (bf16[1,144,768]{2,1,0:T(8,128)(2,1)S(1)}, bf16[1,144,768]{2,1,0:T(8,128)(2,1)S(1)}, u32[]{:S(2)}, u32[]{:S(2)}) collective-permute-start(bf16[1,144,768]{2,1,0:T(8,128)(2,1)S(1)} %get-tuple-element.338), channel_id=1, source_target_pairs={{0,16},{4,20},{8,24},{12,28},{16,0},{20,4},{24,8},{28,12},{1,17},{... | collective-permute-start | bytes 663560 | tf_op jit(solution)/shard_map/ppermute | solution.py:527
  297.9 23.3 %collective-permute-start.21 = (bf16[1,144,768]{2,1,0:T(8,128)(2,1)S(1)}, bf16[1,144,768]{2,1,0:T(8,128)(2,1)S(1)}, u32[]{:S(2)}, u32[]{:S(2)}) collective-permute-start(bf16[1,144,768]{2,1,0:T(8,128)(2,1)S(1)} %get-tuple-element.339), channel_id=1, source_target_pairs={{0,16},{4,20},{8,24},{12,28},{16,0},{20,4},{24,8},{28,12},{1,17},{... | collective-permute-start | bytes 663560 | tf_op jit(solution)/shard_map/ppermute | solution.py:527
  317.4 27.0 %collective-permute-start.16 = (f32[1,8,512]{2,1,0:T(8,128)}, f32[1,8,512]{2,1,0:T(8,128)S(1)}, u32[]{:S(2)}, u32[]{:S(2)}) collective-permute-start(f32[1,8,512]{2,1,0:T(8,128)} %get-tuple-element.162), channel_id=1, source_target_pairs={{0,1},{1,2},{2,3},{3,0},{4,5},{5,6},{6,7},{7,4},{8,9},{9,10},{10,1... | collective-permute-start | bytes 49160 | tf_op jit(solution)/shard_map/ppermute | solution.py:1003
  318.0 29.4 %collective-permute-start.17 = (f32[1,8,512]{2,1,0:T(8,128)}, f32[1,8,512]{2,1,0:T(8,128)S(1)}, u32[]{:S(2)}, u32[]{:S(2)}) collective-permute-start(f32[1,8,512]{2,1,0:T(8,128)} %get-tuple-element.162), channel_id=1, source_target_pairs={{0,2},{1,3},{2,0},{3,1},{4,6},{5,7},{6,4},{7,5},{8,10},{9,11},{10,... | collective-permute-start | bytes 49160 | tf_op jit(solution)/shard_map/ppermute | solution.py:1003
  319.9 28.7 %collective-permute-start.18 = (f32[1,8,512]{2,1,0:T(8,128)}, f32[1,8,512]{2,1,0:T(8,128)S(1)}, u32[]{:S(2)}, u32[]{:S(2)}) collective-permute-start(f32[1,8,512]{2,1,0:T(8,128)} %get-tuple-element.162), channel_id=1, source_target_pairs={{0,3},{1,0},{2,1},{3,2},{4,7},{5,4},{6,5},{7,6},{8,11},{9,8},{10,9... | collective-permute-start | bytes 49160 | tf_op jit(solution)/shard_map/ppermute | solution.py:1003
  329.6 37.6 %collective-permute-start.22 = (f32[1,8,512]{2,1,0:T(8,128)}, f32[1,8,512]{2,1,0:T(8,128)S(1)}, u32[]{:S(2)}, u32[]{:S(2)}) collective-permute-start(f32[1,8,512]{2,1,0:T(8,128)} %get-tuple-element.173), channel_id=1, source_target_pairs={{0,1},{1,2},{2,3},{3,0},{4,5},{5,6},{6,7},{7,4},{8,9},{9,10},{10,1... | collective-permute-start | bytes 49160 | tf_op jit(solution)/shard_map/ppermute | solution.py:1003
  330.4 36.8 %collective-permute-start.23 = (f32[1,8,512]{2,1,0:T(8,128)}, f32[1,8,512]{2,1,0:T(8,128)S(1)}, u32[]{:S(2)}, u32[]{:S(2)}) collective-permute-start(f32[1,8,512]{2,1,0:T(8,128)} %get-tuple-element.173), channel_id=1, source_target_pairs={{0,2},{1,3},{2,0},{3,1},{4,6},{5,7},{6,4},{7,5},{8,10},{9,11},{10,... | collective-permute-start | bytes 49160 | tf_op jit(solution)/shard_map/ppermute | solution.py:1003
  344.4 22.8 %collective-permute-start.24 = (f32[1,8,512]{2,1,0:T(8,128)S(1)}, f32[1,8,512]{2,1,0:T(8,128)S(1)}, u32[]{:S(2)}, u32[]{:S(2)}) collective-permute-start(f32[1,8,512]{2,1,0:T(8,128)S(1)} %copy-done.29), channel_id=1, source_target_pairs={{0,3},{1,0},{2,1},{3,2},{4,7},{5,4},{6,5},{7,6},{8,11},{9,8},{10,9... | collective-permute-start | bytes 49160 | tf_op jit(solution)/shard_map/ppermute | solution.py:1003
  347.4 53.8 %collective-permute-start.32 = (f32[1,8,1024]{2,1,0:T(8,128)}, f32[1,8,1024]{2,1,0:T(8,128)S(1)}, u32[]{:S(2)}, u32[]{:S(2)}) collective-permute-start(f32[1,8,1024]{2,1,0:T(8,128)} %get-tuple-element.199), channel_id=1, source_target_pairs={{4,0},{8,4},{12,8},{16,12},{20,16},{24,20},{28,24},{5,1},{9,5},{13... | collective-permute-start | bytes 98312 | tf_op jit(solution)/shard_map/ppermute | solution.py:1199
  366.0 44.9 %collective-permute-start.33 = (bf16[1,144,768]{2,1,0:T(8,128)(2,1)S(1)}, bf16[1,144,768]{2,1,0:T(8,128)(2,1)S(1)}, u32[]{:S(2)}, u32[]{:S(2)}) collective-permute-start(bf16[1,144,768]{2,1,0:T(8,128)(2,1)S(1)} %pad_maximum_fusion.5), channel_id=1, source_target_pairs={{0,4},{4,0},{8,12},{12,8},{16,20},{20,16},{24,28},{28,24},{1,5},{5... | collective-permute-start | bytes 663560 | tf_op jit(solution)/shard_map/ppermute | solution.py:527
  384.7 26.2 %collective-permute-start.37 = (bf16[1,144,768]{2,1,0:T(8,128)(2,1)S(1)}, bf16[1,144,768]{2,1,0:T(8,128)(2,1)S(1)}, u32[]{:S(2)}, u32[]{:S(2)}) collective-permute-start(bf16[1,144,768]{2,1,0:T(8,128)(2,1)S(1)} %pad_maximum_fusion.6), channel_id=1, source_target_pairs={{0,4},{4,0},{8,12},{12,8},{16,20},{20,16},{24,28},{28,24},{1,5},{5... | collective-permute-start | bytes 663560 | tf_op jit(solution)/shard_map/ppermute | solution.py:527
  (80 other events, 686.4 us)
Sparse Core Ops, SparseCore 0:
  10.7 40.7 all-gather.1
  401.3 320.0 all-reduce.6
